TPU v7x, 256 devices: a whole 4x4x8 slice. The times are simulated.
256 devices in a mesh: gx: 8 (over x, core), gy: 8 (over z), gz: 4 (over y).
Axes of the slice: x: 4, y: 4, z: 8, core: 2. Of those that a mesh axis runs over, the one named last changes fastest.
Arguments:
- gas: float32 [64, 32, 64, 512], P(None, 'gx', 'gy', 'gz'), may hold values from 0 to 1
- droplet: float32 [32, 64, 32768], P(None, None, ('gx', 'gy', 'gz')), may hold values from 0 to 1
- owner: int32 [32768, 1], P(('gx', 'gy', 'gz')), may hold values from 0 to 31; in each aligned block of 128 rows (0 to 127, 128 to 255, ...) at most 8 rows name the same one
- cells: int32 [8, 32768], P(None, ('gx', 'gy', 'gz')), may hold values from 0 to 4095
- weights: float32 [8, 32768], P(None, ('gx', 'gy', 'gz')), may hold values from 0.1 to 1
- mass: float32 [32768], P(('gx', 'gy', 'gz')), may hold values from 0.25 to 4
- liquid_rate: float32 [64], replicated, may hold values from 0.05 to 0.45
- surface_rate: float32 [64], replicated, may hold values from 0.05 to 0.5
- gas_rate: float32 [64], replicated, may hold values from 0.04 to 0.16
Outputs:
- gas_next: float32 [64, 32, 64, 512], P(None, 'gx', 'gy', 'gz')
- droplet_next: float32 [32, 64, 32768], P(None, None, ('gx', 'gy', 'gz'))
Inputs may be any that keep to these rules, and one draw needn't show every extreme that they name: `owner`: among the 128 parcels of one device at most 8 name the same gas device, and some gas device is named by exactly 8 of them.
All inputs are finite; a program needn't handle non-finite values.
Results may differ from a plain program's by a relative error of at most 0.00002.
Values sent between devices are 32-bit elements; how exact they have to be, the bound alone decides.
A program may use at most 64 MiB of HBM per device.

v0:
```python
import jax
import jax.numpy as jnp
from jax import lax
from jax.sharding import PartitionSpec as P

STENCIL = 8
DROP_STEPS = 4
GAS_STEPS = 2


def with_halo(block, sides, width):
    for axis, dim in sides:
        count = lax.axis_size(axis)
        forward = [(i, i + 1) for i in range(count - 1)]
        backward = [(target, source) for source, target in forward]
        low = lax.ppermute(
            lax.slice_in_dim(block, block.shape[dim] - width, None, axis=dim), axis, forward
        )
        high = lax.ppermute(lax.slice_in_dim(block, 0, width, axis=dim), axis, backward)
        block = jnp.concatenate([low, block, high], axis=dim)
    return block


def droplet_steps(state, gas_at, liquid_rate, surface_rate):
    liquid_coef = liquid_rate[None, :, None]
    surface_coef = surface_rate[:, None]
    emitted = jnp.zeros(gas_at.shape, jnp.float32)
    for substep in range(DROP_STEPS):
        surface_flux = surface_coef * (state[-1] - gas_at)
        upper_node = jnp.concatenate([state[1:], state[-1:]], axis=0)
        lower_node = jnp.concatenate([state[1:2], state[:-1]], axis=0)
        state = state + liquid_coef * (upper_node - 2.0 * state + lower_node)
        state = state.at[-1].add(-surface_flux)
        emitted = emitted + surface_flux
    return (state, emitted)


def stencil_update(padded, field, gas_rate):
    beside = padded[:, 2:, 1:-1, 1:-1] + padded[:, :-2, 1:-1, 1:-1]
    beside = beside + padded[:, 1:-1, 2:, 1:-1] + padded[:, 1:-1, :-2, 1:-1]
    beside = beside + padded[:, 1:-1, 1:-1, 2:] + padded[:, 1:-1, 1:-1, :-2]
    return field + gas_rate[:, None, None, None] * (beside - 6.0 * field)


def gas_step(field, gas_rate):
    padded = with_halo(field, (("gx", 1), ("gy", 2), ("gz", 3)), 1)
    return stencil_update(padded, field, gas_rate)


def on_device(gas, droplet, owner, cells, weights, mass, liquid_rate, surface_rate, gas_rate):
    span_first = lax.axis_size("gy")
    span_second = lax.axis_size("gz")
    group_size = span_first * span_second
    parcels = droplet.shape[2]
    capacity = 2 * parcels // group_size
    species = gas.shape[0]
    norm_wts = weights / jnp.sum(weights, axis=0, keepdims=True)
    target = owner[:, 0]
    onehot = (target[:, None] == jnp.arange(group_size, dtype=jnp.int32)[None, :]).astype(jnp.int32)
    slot_rank = jnp.sum(onehot * (jnp.cumsum(onehot, axis=0) - 1), axis=1)
    slot_index = target * capacity + slot_rank
    send_ids = jnp.zeros((STENCIL, group_size * capacity), jnp.int32).at[:, slot_index].set(cells)
    send_ids = send_ids.reshape(STENCIL, group_size, capacity)
    send_wts = (
        jnp.zeros((STENCIL, group_size * capacity), jnp.float32).at[:, slot_index].set(norm_wts)
    )
    send_wts = send_wts.reshape(STENCIL, group_size, capacity)
    gasflat = gas.reshape(species, -1)
    cell_ids = lax.all_to_all(send_ids, ("gy", "gz"), split_axis=1, concat_axis=1, tiled=True)
    cell_wts = lax.all_to_all(send_wts, ("gy", "gz"), split_axis=1, concat_axis=1, tiled=True)
    values = gasflat[:, cell_ids.reshape(-1)].reshape((species,) + cell_ids.shape)
    row_values = jnp.sum(cell_wts[None] * values, axis=1)
    returned = lax.all_to_all(row_values, ("gy", "gz"), split_axis=1, concat_axis=1, tiled=True)
    gas_at = returned.reshape(species, -1)[:, slot_index]
    droplet_next, emitted = droplet_steps(droplet, gas_at, liquid_rate, surface_rate)
    source = mass[None, :] * emitted
    send_source = (
        jnp.zeros((species, group_size * capacity), jnp.float32).at[:, slot_index].set(source)
    )
    recv_source = lax.all_to_all(
        send_source.reshape(species, group_size, capacity),
        ("gy", "gz"),
        split_axis=1,
        concat_axis=1,
        tiled=True,
    )
    field = gas
    for substep in range(GAS_STEPS):
        field = gas_step(field, gas_rate)
    flat_out = field.reshape(species, -1)
    deposit = (cell_wts[None] * recv_source[:, None]).reshape(species, -1)
    flat_out = flat_out.at[:, cell_ids.reshape(-1)].add(deposit)
    return (flat_out.reshape(gas.shape), droplet_next)


def solution(mesh):
    return jax.shard_map(
        on_device,
        mesh=mesh,
        in_specs=(
            P(None, "gx", "gy", "gz"),
            P(None, None, ("gx", "gy", "gz")),
            P(("gx", "gy", "gz"), None),
            P(None, ("gx", "gy", "gz")),
            P(None, ("gx", "gy", "gz")),
            P(("gx", "gy", "gz")),
            P(),
            P(),
            P(),
        ),
        out_specs=(P(None, "gx", "gy", "gz"), P(None, None, ("gx", "gy", "gz"))),
        check_vma=False,
    )
```

profile of v0, /device:TPU:2, one launch (start us, length us, event | category | flops | bytes accessed | tf_op | source)
XLA Modules:
  0.0 190.6 jit_solution(1585852194268087470)
XLA Ops:
  5.6 11.5 %all-to-all-start = ((s32[8,32,8]{2,0,1:T(8,128)}), s32[8,32,8]{2,0,1:T(8,128)S(1)}, u32[]{:S(2)}, u32[]{:S(2)}) async-start(s32[8,32,8]{2,0,1:T(8,128)} %copy.55), calls=%async_computation | async-start | bytes 262144 | tf_op jit(solution)/shard_map/all_to_all | solution.py:69
  21.8 3.6 %collective-permute-start = (f32[64,1,8,128]{3,0,2,1:T(8,128)}, f32[64,1,8,128]{3,0,2,1:T(8,128)}, u32[]{:S(2)}, u32[]{:S(2)}) collective-permute-start(f32[64,1,8,128]{3,0,2,1:T(8,128)} %get-tuple-element.82), channel_id=1, source_target_pairs={{32,0},{64,32},{96,64},{128,96},{160,128},{192,160},{224,192},{33,... | collective-permute-start | bytes 786440 | tf_op jit(solution)/shard_map/ppermute | solution.py:19
  26.1 2.5 %fusion.65 = (f32[31,64,128]{1,2,0:T(8,128)}, f32[31,64,128]{1,2,0:T(8,128)}) fusion(f32[32,64,128]{1,2,0:T(8,128)S(1)} %copy.60), kind=kLoop, calls=%fused_computation.133 | loop fusion | bytes 4063232 | tf_op jit(solution)/shard_map/slice | solution.py:31
  33.1 9.8 %all-to-all-start.1 = ((f32[8,32,8]{2,0,1:T(8,128)}), f32[8,32,8]{2,0,1:T(8,128)S(1)}, u32[]{:S(2)}, u32[]{:S(2)}) async-start(f32[8,32,8]{2,0,1:T(8,128)} %copy.58), calls=%async_computation.1 | async-start | bytes 262144 | tf_op jit(solution)/shard_map/all_to_all | solution.py:70
  43.1 9.3 %gather_fusion = f32[2048,64]{1,0:T(8,128)} fusion(f32[64,4096]{0,1:T(8,128)} %bitcast.109, s32[2048]{0:T(1024)S(1)} %broadcast_clamp_fusion), kind=kCustom, calls=%fused_computation | custom fusion | bytes 1056768 | tf_op jit(solution)/shard_map/gather | solution.py:71
  55.7 8.8 %all-to-all-start.2 = ((f32[32,1,512]{2,1,0:T(1,128)}), f32[32,1,512]{2,1,0:T(1,128)S(1)}, u32[]{:S(2)}, u32[]{:S(2)}) async-start(f32[32,1,512]{2,1,0:T(1,128)} %reshape.268), calls=%async_computation.2 | async-start | bytes 131072 | tf_op jit(solution)/shard_map/all_to_all | solution.py:73
  64.6 4.2 %fusion.2 = f32[32,64,128]{1,2,0:T(8,128)} fusion(f32[32,64,128]{1,2,0:T(8,128)S(1)} %copy.60, f32[1,64,128]{1,2,0:T(8,128)S(1)} %copy-done.12, f32[31,64,128]{1,2,0:T(8,128)} %get-tuple-element.71, f32[31,64,128]{1,2,0:T(8,128)} %get-tuple-element.70, f32[1,64,128]{1,2,0:T(8,128)S(1)} %copy-done.11, f32[64]{0:T(128)S(1)} %copy-done.15), kind=kLoop, calls=%fused_computation.9 | loop fusion | flops 1835008 | bytes 4194560 | tf_op jit(solution)/shard_map/add | solution.py:32
  68.9 5.7 %all-to-all-done.2 = f32[32,1,512]{2,1,0:T(1,128)S(1)} async-done(((f32[32,1,512]{2,1,0:T(1,128)}), f32[32,1,512]{2,1,0:T(1,128)S(1)}, u32[]{:S(2)}, u32[]{:S(2)}) %all-to-all-start.2) | async-done | bytes 65568 | tf_op jit(solution)/shard_map/all_to_all | solution.py:73
  78.1 2.6 %fusion.63 = (f32[31,64,128]{1,2,0:T(8,128)S(1)}, f32[31,64,128]{1,2,0:T(8,128)S(1)}) fusion(f32[32,64,128]{1,2,0:T(8,128)} %get-tuple-element.60), kind=kLoop, calls=%fused_computation.131 | loop fusion | bytes 4063232 | tf_op jit(solution)/shard_map/slice | solution.py:31
  89.4 4.6 %collective-permute-start.3 = (f32[64,6,1,128]{3,0,2,1:T(8,128)S(1)}, f32[64,6,1,128]{3,0,2,1:T(8,128)S(1)}, u32[]{:S(2)}, u32[]{:S(2)}) collective-permute-start(f32[64,6,1,128]{3,0,2,1:T(8,128)S(1)} %get-tuple-element.78), channel_id=1, source_target_pairs={{0,4},{4,8},{8,12},{12,16},{16,20},{20,24},{24,28},{1,5},{5,9},{9,... | collective-permute-start | bytes 589832 | tf_op jit(solution)/shard_map/ppermute | solution.py:16
  105.5 4.6 %collective-permute-start.5 = (f32[64,6,10,1]{0,1,3,2:T(8,128)S(1)}, f32[64,6,10,1]{0,1,3,2:T(8,128)S(1)}, u32[]{:S(2)}, u32[]{:S(2)}) collective-permute-start(f32[64,6,10,1]{0,1,3,2:T(8,128)S(1)} %copy.45), channel_id=1, source_target_pairs={{0,1},{1,2},{2,3},{4,5},{5,6},{6,7},{8,9},{9,10},{10,11},{12,13},{... | collective-permute-start | bytes 46088 | tf_op jit(solution)/shard_map/ppermute | solution.py:16
  112.3 7.7 %all-to-all-start.3 = ((f32[32,1,512]{2,1,0:T(1,128)}), f32[32,1,512]{2,1,0:T(1,128)}, u32[]{:S(2)}, u32[]{:S(2)}) async-start(f32[32,1,512]{2,1,0:T(1,128)} %reshape.270), calls=%async_computation.3 | async-start | bytes 131072 | tf_op jit(solution)/shard_map/all_to_all | solution.py:80
  123.9 3.7 %fusion.23 = f32[64,4,8,128]{3,0,2,1:T(8,128)S(1)} fusion(f32[64,4,8,128]{3,0,2,1:T(8,128)} %copy-done.4, f32[64,6,10,1]{3,0,2,1:T(8,128)} %copy.46, f32[64,6,1,128]{3,0,2,1:T(8,128)S(1)} %collective-permute-done.2, f32[64,6,8,128]{3,0,2,1:T(8,128)S(1)} %copy-done.3, f32[64,6,1,128]{3,0,2,1:T(8,128)S(1)} %collective-permute-done.3, ...), kind=kLoop, calls=%fused_computation.54 | loop fusion | flops 4980736 | bytes 4618496 | tf_op jit(solution)/shard_map/add | solution.py:42
  129.6 2.5 %collective-permute-start.7 = (f32[64,1,8,128]{3,0,2,1:T(8,128)S(1)}, f32[64,1,8,128]{3,0,2,1:T(8,128)S(1)}, u32[]{:S(2)}, u32[]{:S(2)}) collective-permute-start(f32[64,1,8,128]{3,0,2,1:T(8,128)S(1)} %get-tuple-element.80), channel_id=1, source_target_pairs={{0,32},{32,64},{64,96},{96,128},{128,160},{160,192},{192,224},{1,3... | collective-permute-start | bytes 786440 | tf_op jit(solution)/shard_map/ppermute | solution.py:16
  132.1 2.4 %fusion.61 = (f32[31,64,128]{1,2,0:T(8,128)S(1)}, f32[31,64,128]{1,2,0:T(8,128)S(1)}) fusion(f32[32,64,128]{1,2,0:T(8,128)} %get-tuple-element.56), kind=kLoop, calls=%fused_computation.129 | loop fusion | bytes 4063232 | tf_op jit(solution)/shard_map/slice | solution.py:31
  134.6 2.8 %collective-permute-done.7 = f32[64,1,8,128]{3,0,2,1:T(8,128)S(1)} collective-permute-done((f32[64,1,8,128]{3,0,2,1:T(8,128)S(1)}, f32[64,1,8,128]{3,0,2,1:T(8,128)S(1)}, u32[]{:S(2)}, u32[]{:S(2)}) %collective-permute-start.7) | collective-permute-done | bytes 262176 | tf_op jit(solution)/shard_map/ppermute | solution.py:16
  138.7 4.6 %collective-permute-start.9 = (f32[64,6,1,128]{3,0,2,1:T(8,128)S(1)}, f32[64,6,1,128]{3,0,2,1:T(8,128)S(1)}, u32[]{:S(2)}, u32[]{:S(2)}) collective-permute-start(f32[64,6,1,128]{3,0,2,1:T(8,128)S(1)} %get-tuple-element.76), channel_id=1, source_target_pairs={{0,4},{4,8},{8,12},{12,16},{16,20},{20,24},{24,28},{1,5},{5,9},{9,... | collective-permute-start | bytes 589832 | tf_op jit(solution)/shard_map/ppermute | solution.py:16
  146.6 2.6 %fusion.66 = (f32[64,6,10,1]{3,0,2,1:T(8,128)}, f32[64,6,10,1]{3,0,2,1:T(8,128)}) fusion(f32[64,6,10,128]{3,0,2,1:T(8,128)S(1)} %pad_maximum_fusion.1), kind=kLoop, calls=%fused_computation.134 | loop fusion | bytes 61440 | tf_op jit(solution)/shard_map/slice | solution.py:19
  149.2 3.0 %copy.49 = f32[64,6,10,1]{0,1,3,2:T(8,128)} copy(f32[64,6,10,1]{3,0,2,1:T(8,128)} %get-tuple-element.72) | data formatting | bytes 30720 | tf_op jit(solution)/shard_map/slice | solution.py:19
  153.5 3.0 %copy.51 = f32[64,6,10,1]{0,1,3,2:T(8,128)} copy(f32[64,6,10,1]{3,0,2,1:T(8,128)} %get-tuple-element.73) | data formatting | bytes 30720 | tf_op jit(solution)/shard_map/slice | solution.py:17
  156.5 5.1 %collective-permute-start.11 = (f32[64,6,10,1]{0,1,3,2:T(8,128)}, f32[64,6,10,1]{0,1,3,2:T(8,128)}, u32[]{:S(2)}, u32[]{:S(2)}) collective-permute-start(f32[64,6,10,1]{0,1,3,2:T(8,128)} %copy.51), channel_id=1, source_target_pairs={{0,1},{1,2},{2,3},{4,5},{5,6},{6,7},{8,9},{9,10},{10,11},{12,13},{... | collective-permute-start | bytes 46088 | tf_op jit(solution)/shard_map/ppermute | solution.py:16
  168.3 2.7 %copy.52 = f32[64,6,10,1]{3,0,2,1:T(8,128)} copy(f32[64,6,10,1]{0,1,3,2:T(8,128)} %collective-permute-done.11) | data formatting | bytes 30720 | tf_op jit(solution)/shard_map/ppermute | solution.py:16
  171.1 3.6 %fusion.15 = f32[64,4,8,128]{3,0,2,1:T(8,128)} fusion(f32[64,4,8,128]{3,0,2,1:T(8,128)S(1)} %fusion.23, f32[64,6,10,1]{3,0,2,1:T(8,128)} %copy.52, f32[64,6,1,128]{3,0,2,1:T(8,128)} %copy-done.8, f32[64,6,1,128]{3,0,2,1:T(8,128)} %copy-done.9, f32[64,1,8,128]{3,0,2,1:T(8,128)S(1)} %collective-permute-done.6, f32[64,1,8,128]{3,0,2,1:T(8,128)} %copy-done.6, ...), kind=kLoop, calls=%fused_computation.28 | loop fusion | flops 7077888 | bytes 3045632 | tf_op jit(solution)/shard_map/add | solution.py:42
  176.6 12.3 %scatter_custom_fusion.3 = f32[64,4096]{0,1:T(8,128)S(1)} fusion(f32[64,4096]{0,1:T(8,128)S(1)} %bitcast.110, s32[2048]{0:T(1024)S(1)} %bitcast.118, f32[64,2048]{0,1:T(8,128)S(1)} %copy-done.5), kind=kCustom, calls=%fused_computation.68 | custom fusion | flops 131072 | bytes 2097152 | tf_op jit(solution)/shard_map/scatter-add | solution.py:92
  (127 shorter events, 66.3 us)
Async XLA Ops:
  0.6 24.8 %copy-start.7 = (f32[32,64,128]{2,1,0:T(8,128)S(1)}, f32[32,64,128]{2,1,0:T(8,128)}, u32[]{:S(2)}) copy-start(f32[32,64,128]{2,1,0:T(8,128)} %param.18) | copy-start | bytes 3145732
  3.1 65.6 %copy-start.20 = (s32[128]{0:T(128)}, s32[128]{0:T(128)S(1)}, u32[]{:S(2)}) copy-start(s32[128]{0:T(128)S(1)} %fusion.59) | copy-start | bytes 1540
  5.6 27.5 %all-to-all-start = ((s32[8,32,8]{2,0,1:T(8,128)}), s32[8,32,8]{2,0,1:T(8,128)S(1)}, u32[]{:S(2)}, u32[]{:S(2)}) async-start(s32[8,32,8]{2,0,1:T(8,128)} %copy.55), calls=%async_computation | async-start | bytes 262144 | tf_op jit(solution)/shard_map/all_to_all | solution.py:69
  19.9 64.5 %collective-permute-start.1 = (f32[64,1,8,128]{3,0,2,1:T(8,128)}, f32[64,1,8,128]{3,0,2,1:T(8,128)}, u32[]{:S(2)}, u32[]{:S(2)}) collective-permute-start(f32[64,1,8,128]{3,0,2,1:T(8,128)} %get-tuple-element.83), channel_id=1, source_target_pairs={{0,32},{32,64},{64,96},{96,128},{128,160},{160,192},{192,224},{1,3... | collective-permute-start | bytes 786440 | tf_op jit(solution)/shard_map/ppermute | solution.py:16
  21.8 64.2 %collective-permute-start = (f32[64,1,8,128]{3,0,2,1:T(8,128)}, f32[64,1,8,128]{3,0,2,1:T(8,128)}, u32[]{:S(2)}, u32[]{:S(2)}) collective-permute-start(f32[64,1,8,128]{3,0,2,1:T(8,128)} %get-tuple-element.82), channel_id=1, source_target_pairs={{32,0},{64,32},{96,64},{128,96},{160,128},{192,160},{224,192},{33,... | collective-permute-start | bytes 786440 | tf_op jit(solution)/shard_map/ppermute | solution.py:19
  33.1 20.2 %all-to-all-start.1 = ((f32[8,32,8]{2,0,1:T(8,128)}), f32[8,32,8]{2,0,1:T(8,128)S(1)}, u32[]{:S(2)}, u32[]{:S(2)}) async-start(f32[8,32,8]{2,0,1:T(8,128)} %copy.58), calls=%async_computation.1 | async-start | bytes 262144 | tf_op jit(solution)/shard_map/all_to_all | solution.py:70
  43.1 21.5 %copy-start.11 = (f32[1,64,128]{1,2,0:T(8,128)S(1)}, f32[1,64,128]{1,2,0:T(8,128)}, u32[]{:S(2)}) copy-start(f32[1,64,128]{1,2,0:T(8,128)} %get-tuple-element.68) | copy-start | bytes 98308
  43.1 21.5 %copy-start.12 = (f32[1,64,128]{1,2,0:T(8,128)S(1)}, f32[1,64,128]{1,2,0:T(8,128)}, u32[]{:S(2)}) copy-start(f32[1,64,128]{1,2,0:T(8,128)} %get-tuple-element.69) | copy-start | bytes 98308
  43.1 21.5 %copy-start.15 = (f32[64]{0:T(128)S(1)}, f32[64]{0:T(128)}, u32[]{:S(2)}) copy-start(f32[64]{0:T(128)} %param.23) | copy-start | bytes 772
  55.7 18.8 %all-to-all-start.2 = ((f32[32,1,512]{2,1,0:T(1,128)}), f32[32,1,512]{2,1,0:T(1,128)S(1)}, u32[]{:S(2)}, u32[]{:S(2)}) async-start(f32[32,1,512]{2,1,0:T(1,128)} %reshape.268), calls=%async_computation.2 | async-start | bytes 131072 | tf_op jit(solution)/shard_map/all_to_all | solution.py:73
  88.1 8.6 %collective-permute-start.2 = (f32[64,6,1,128]{3,0,2,1:T(8,128)S(1)}, f32[64,6,1,128]{3,0,2,1:T(8,128)S(1)}, u32[]{:S(2)}, u32[]{:S(2)}) collective-permute-start(f32[64,6,1,128]{3,0,2,1:T(8,128)S(1)} %get-tuple-element.79), channel_id=1, source_target_pairs={{4,0},{8,4},{12,8},{16,12},{20,16},{24,20},{28,24},{5,1},{9,5},{13... | collective-permute-start | bytes 589832 | tf_op jit(solution)/shard_map/ppermute | solution.py:19
  89.4 7.7 %collective-permute-start.3 = (f32[64,6,1,128]{3,0,2,1:T(8,128)S(1)}, f32[64,6,1,128]{3,0,2,1:T(8,128)S(1)}, u32[]{:S(2)}, u32[]{:S(2)}) collective-permute-start(f32[64,6,1,128]{3,0,2,1:T(8,128)S(1)} %get-tuple-element.78), channel_id=1, source_target_pairs={{0,4},{4,8},{8,12},{12,16},{16,20},{20,24},{24,28},{1,5},{5,9},{9,... | collective-permute-start | bytes 589832 | tf_op jit(solution)/shard_map/ppermute | solution.py:16
  103.1 16.9 %collective-permute-start.4 = (f32[64,6,10,1]{0,1,3,2:T(8,128)S(1)}, f32[64,6,10,1]{0,1,3,2:T(8,128)S(1)}, u32[]{:S(2)}, u32[]{:S(2)}) collective-permute-start(f32[64,6,10,1]{0,1,3,2:T(8,128)S(1)} %copy.43), channel_id=1, source_target_pairs={{1,0},{2,1},{3,2},{5,4},{6,5},{7,6},{9,8},{10,9},{11,10},{13,12},{... | collective-permute-start | bytes 46088 | tf_op jit(solution)/shard_map/ppermute | solution.py:19
  105.5 16.5 %collective-permute-start.5 = (f32[64,6,10,1]{0,1,3,2:T(8,128)S(1)}, f32[64,6,10,1]{0,1,3,2:T(8,128)S(1)}, u32[]{:S(2)}, u32[]{:S(2)}) collective-permute-start(f32[64,6,10,1]{0,1,3,2:T(8,128)S(1)} %copy.45), channel_id=1, source_target_pairs={{0,1},{1,2},{2,3},{4,5},{5,6},{6,7},{8,9},{9,10},{10,11},{12,13},{... | collective-permute-start | bytes 46088 | tf_op jit(solution)/shard_map/ppermute | solution.py:16
  112.3 11.6 %copy-start.18 = (f32[64]{0:T(128)S(1)}, f32[64]{0:T(128)}, u32[]{:S(2)}) copy-start(f32[64]{0:T(128)} %param.25) | copy-start | bytes 772
  112.3 51.6 %all-to-all-start.3 = ((f32[32,1,512]{2,1,0:T(1,128)}), f32[32,1,512]{2,1,0:T(1,128)}, u32[]{:S(2)}, u32[]{:S(2)}) async-start(f32[32,1,512]{2,1,0:T(1,128)} %reshape.270), calls=%async_computation.3 | async-start | bytes 131072 | tf_op jit(solution)/shard_map/all_to_all | solution.py:80
  127.6 7.0 %collective-permute-start.6 = (f32[64,1,8,128]{3,0,2,1:T(8,128)S(1)}, f32[64,1,8,128]{3,0,2,1:T(8,128)S(1)}, u32[]{:S(2)}, u32[]{:S(2)}) collective-permute-start(f32[64,1,8,128]{3,0,2,1:T(8,128)S(1)} %get-tuple-element.81), channel_id=1, source_target_pairs={{32,0},{64,32},{96,64},{128,96},{160,128},{192,160},{224,192},{33,... | collective-permute-start | bytes 786440 | tf_op jit(solution)/shard_map/ppermute | solution.py:19
  129.6 13.7 %copy-start.10 = (f32[1,64,128]{1,2,0:T(8,128)S(1)}, f32[1,64,128]{1,2,0:T(8,128)}, u32[]{:S(2)}) copy-start(f32[1,64,128]{1,2,0:T(8,128)} %slice.287) | copy-start | bytes 98308
  129.6 13.7 %copy-start.17 = (f32[64]{0:T(128)S(1)}, f32[64]{0:T(128)}, u32[]{:S(2)}) copy-start(f32[64]{0:T(128)} %param.23) | copy-start | bytes 772
  129.6 7.8 %collective-permute-start.7 = (f32[64,1,8,128]{3,0,2,1:T(8,128)S(1)}, f32[64,1,8,128]{3,0,2,1:T(8,128)S(1)}, u32[]{:S(2)}, u32[]{:S(2)}) collective-permute-start(f32[64,1,8,128]{3,0,2,1:T(8,128)S(1)} %get-tuple-element.80), channel_id=1, source_target_pairs={{0,32},{32,64},{64,96},{96,128},{128,160},{160,192},{192,224},{1,3... | collective-permute-start | bytes 786440 | tf_op jit(solution)/shard_map/ppermute | solution.py:16
  137.4 8.2 %collective-permute-start.8 = (f32[64,6,1,128]{3,0,2,1:T(8,128)S(1)}, f32[64,6,1,128]{3,0,2,1:T(8,128)S(1)}, u32[]{:S(2)}, u32[]{:S(2)}) collective-permute-start(f32[64,6,1,128]{3,0,2,1:T(8,128)S(1)} %get-tuple-element.77), channel_id=1, source_target_pairs={{4,0},{8,4},{12,8},{16,12},{20,16},{24,20},{28,24},{5,1},{9,5},{13... | collective-permute-start | bytes 589832 | tf_op jit(solution)/shard_map/ppermute | solution.py:19
  138.7 7.7 %collective-permute-start.9 = (f32[64,6,1,128]{3,0,2,1:T(8,128)S(1)}, f32[64,6,1,128]{3,0,2,1:T(8,128)S(1)}, u32[]{:S(2)}, u32[]{:S(2)}) collective-permute-start(f32[64,6,1,128]{3,0,2,1:T(8,128)S(1)} %get-tuple-element.76), channel_id=1, source_target_pairs={{0,4},{4,8},{8,12},{12,16},{16,20},{20,24},{24,28},{1,5},{5,9},{9,... | collective-permute-start | bytes 589832 | tf_op jit(solution)/shard_map/ppermute | solution.py:16
  152.2 14.7 %collective-permute-start.10 = (f32[64,6,10,1]{0,1,3,2:T(8,128)}, f32[64,6,10,1]{0,1,3,2:T(8,128)}, u32[]{:S(2)}, u32[]{:S(2)}) collective-permute-start(f32[64,6,10,1]{0,1,3,2:T(8,128)} %copy.49), channel_id=1, source_target_pairs={{1,0},{2,1},{3,2},{5,4},{6,5},{7,6},{9,8},{10,9},{11,10},{13,12},{... | collective-permute-start | bytes 46088 | tf_op jit(solution)/shard_map/ppermute | solution.py:19
  156.5 11.9 %collective-permute-start.11 = (f32[64,6,10,1]{0,1,3,2:T(8,128)}, f32[64,6,10,1]{0,1,3,2:T(8,128)}, u32[]{:S(2)}, u32[]{:S(2)}) collective-permute-start(f32[64,6,10,1]{0,1,3,2:T(8,128)} %copy.51), channel_id=1, source_target_pairs={{0,1},{1,2},{2,3},{4,5},{5,6},{6,7},{8,9},{9,10},{10,11},{12,13},{... | collective-permute-start | bytes 46088 | tf_op jit(solution)/shard_map/ppermute | solution.py:16
  (13 other events, 50.0 us)
where the time goes:
time: 193 us; the launch traced here: 191 us
  starting transfers between devices  72 us (37%)
  local copies, waits for them, and re-layouts  63.4 us (33%)
  other arithmetic  43.3 us (22%)
  waiting for transfers between devices  10.7 us (6%)
    ppermute x6, starting transfers between devices, with_halo(): lax.ppermute(lax.slice_in_dim(block, block.shape[dim] - width, None, axis...  23.3 us
    unnamed x55, local copies, waits for them, and re-layouts  13.3 us
    scatter-add x1, other arithmetic, on_device(): flat_out = flat_out.at[:, cell_ids.reshape(-1)].add(deposit)  12.3 us
    all_to_all x1, starting transfers between devices, on_device(): lax.all_to_all(send_ids, ('gy', 'gz'), split_axis=1, concat_axis=1, tiled...  11.5 us
    ppermute x6, starting transfers between devices, with_halo(): lax.ppermute(lax.slice_in_dim(block, 0, width, axis=dim), axis, backward)  10.9 us
    slice x5, local copies, waits for them, and re-layouts, with_halo(): lax.slice_in_dim(block, 0, width, axis=dim)  10.9 us
    slice x8, local copies, waits for them, and re-layouts, droplet_steps(): lower_node = jnp.concatenate([state[1:2], state[:-1]], axis=0)  10.2 us
    all_to_all x1, starting transfers between devices, on_device(): lax.all_to_all(send_wts, ('gy', 'gz'), split_axis=1, concat_axis=1, tiled...  9.78 us
  transfers between devices with their start and end apart: 16, of which 5 were waited for; matrix products, arithmetic and copies ran while one was open for 37% of the time, Pallas kernels for 0%

commit v1 on v0

v1 whole, which is shorter than its diff:
```python
import functools

import jax
import jax.numpy as jnp
from jax import lax
from jax.experimental import pallas as pl
from jax.experimental.pallas import tpu as pltpu
from jax.sharding import PartitionSpec as P

STENCIL = 8
DROP_STEPS = 4
MESH = pl.DeviceIdType.MESH
F32 = jnp.float32
BF16 = jnp.bfloat16
EXACT = lax.Precision.HIGHEST
NT = (((1,), (1,)), ((), ()))
NN = (((1,), (0,)), ((), ()))


def iota(shape, dim):
    return lax.broadcasted_iota(jnp.int32, shape, dim)


def column(row, lanes=None):
    n = row.shape[1]
    spread = jnp.broadcast_to(row, (n, n))
    picked = jnp.where(iota((n, n), 0) == iota((n, n), 1), spread, jnp.zeros_like(spread))
    return jnp.sum(picked, axis=1, keepdims=True)


def split(value):
    high = value.astype(BF16)
    low = (value - high.astype(F32)).astype(BF16)
    return high, low


def exact_dot(a, b, dims):
    return lax.dot_general(a, b, dims, precision=EXACT, preferred_element_type=F32)


def dot(a, b, dims):
    return lax.dot_general(a, b, dims, preferred_element_type=F32)


def kernel(
    n_gx, n_gy, n_gz, nx, ny,
    gas, droplet, owner, cells, weights, mass, liquid, surface, gasrate,
    gas_out, drop_out,
    raw, first, second, parts, drop, lam_b, sig_b, gam_b, reply_b, emit_b,
    w_hi, w_lo, zk_s, rk_s, vh_s, vl_s, acc_s, acc2_s, out_s,
    meta_send, meta_recv, base_send, base_recv, back_send, back_recv,
    edge_send, edge_recv,
    in_sem, out_sem,
    meta_ssem, meta_rsem, base_ssem, base_rsem, back_ssem, back_rsem,
    face_ssem, face_rsem,
):
    group = n_gy * n_gz
    rows = nx * ny
    half = 4 * group
    species = liquid.shape[1]
    nodes = droplet.shape[0]
    parcels = owner.shape[1]
    cz = 128

    gx = lax.axis_index("gx")
    gy = lax.axis_index("gy")
    gz = lax.axis_index("gz")
    me = gy * n_gz + gz

    def peer_id(o):
        return {"gy": o // n_gz, "gz": lax.rem(o, n_gz)}

    gas_in = pltpu.make_async_copy(gas, raw, in_sem.at[0])
    gas_in.start()
    drop_in = pltpu.make_async_copy(droplet, drop, in_sem.at[1])
    drop_in.start()

    barrier = pltpu.get_barrier_semaphore()

    def greet(j, carry):
        o = lax.rem(me + j, group)
        pl.semaphore_signal(barrier, inc=1, device_id=peer_id(o), device_id_type=MESH)
        return carry

    lax.fori_loop(1, group, greet, 0)
    for step in (1, n_gx - 1):
        pl.semaphore_signal(
            barrier, inc=1, device_id={"gx": lax.rem(gx + step, n_gx)}, device_id_type=MESH
        )

    own = owner[...]
    own_col = column(own)
    before = (own_col == own) & (iota((parcels, parcels), 0) < iota((parcels, parcels), 1))
    rank = jnp.sum(before.astype(F32), axis=0, keepdims=True).astype(jnp.int32)
    onehot = (iota((group, parcels), 0) == own).astype(F32)
    slot = (iota((8, parcels), 0) == rank).astype(F32)
    wts = weights[...]
    wts = wts / jnp.sum(wts, axis=0, keepdims=True)
    wts = wts * mass[...]
    cell = cells[...]
    cell_f = cell.astype(F32)
    tiles = [cell_f[q:q + 1] * slot for q in range(STENCIL)]
    tiles += [wts[q:q + 1] * slot for q in range(STENCIL)]
    spread = jnp.concatenate(tiles, axis=0)
    meta_send[...] = exact_dot(onehot, spread, NT)

    pl.semaphore_wait(barrier, group + 1)

    def exchange(src_of, dst_of, ssem, rsem):
        def send(j, carry):
            o = lax.rem(me + j, group)
            pltpu.make_async_remote_copy(
                src_ref=src_of(o), dst_ref=dst_of(me), send_sem=ssem.at[o], recv_sem=rsem.at[me],
                device_id=peer_id(o), device_id_type=MESH,
            ).start()
            return carry

        lax.fori_loop(1, group, send, 0)
        pltpu.make_async_copy(src_of(me), dst_of(me), rsem.at[me]).start()

    def await_recv(dst_of, rsem):
        def take(o, carry):
            pltpu.make_async_copy(dst_of(o), dst_of(o), rsem.at[o]).wait()
            return carry

        lax.fori_loop(0, group, take, 0)

    def await_send(src_of, ssem):
        def take(j, carry):
            o = lax.rem(me + j, group)
            pltpu.make_async_copy(src_of(o), src_of(o), ssem.at[o]).wait()
            return carry

        lax.fori_loop(1, group, take, 0)

    meta_row = lambda ref: (lambda o: ref.at[pl.ds(o, 1)])
    slab_row = lambda ref: (lambda o: ref.at[:, pl.ds(o, 1)])

    exchange(meta_row(meta_send), meta_row(meta_recv), meta_ssem, meta_rsem)

    def faces(buf, step):
        inner_x, inner_y = pl.ds(1, nx), pl.ds(1, ny)
        table = [
            (gx > 0, {"gx": gx - 1}, buf.at[1, inner_y], buf.at[nx + 1, inner_y], gx < n_gx - 1),
            (gx < n_gx - 1, {"gx": gx + 1}, buf.at[nx, inner_y], buf.at[0, inner_y], gx > 0),
            (gy > 0, {"gy": gy - 1}, buf.at[inner_x, 1], buf.at[inner_x, ny + 1], gy < n_gy - 1),
            (gy < n_gy - 1, {"gy": gy + 1}, buf.at[inner_x, ny], buf.at[inner_x, 0], gy > 0),
            (gz > 0, {"gz": gz - 1}, edge_send.at[step], edge_recv.at[step, 1], gz < n_gz - 1),
            (gz < n_gz - 1, {"gz": gz + 1}, edge_send.at[step], edge_recv.at[step, 0], gz > 0),
        ]
        out = []
        for i, (send_if, target, src, dst, recv_if) in enumerate(table):
            copy = pltpu.make_async_remote_copy(
                src_ref=src, dst_ref=dst, send_sem=face_ssem.at[step, i],
                recv_sem=face_rsem.at[step, i], device_id=target, device_id_type=MESH,
            )
            out.append((send_if, copy, recv_if, dst))
        return out

    def start_faces(buf, step):
        for send_if, copy, _, _ in faces(buf, step):
            pl.when(send_if)(copy.start)

    def await_faces(buf, step):
        for i, (_, _, recv_if, dst) in enumerate(faces(buf, step)):
            wait = pltpu.make_async_copy(dst, dst, face_rsem.at[step, i]).wait
            pl.when(recv_if)(wait)

    def drain_faces(buf, step):
        for send_if, copy, _, _ in faces(buf, step):
            pl.when(send_if)(copy.wait_send)

    def outside_zero(buf, step):
        zero_x = jnp.zeros((ny, species, cz), F32)
        zero_y = jnp.zeros((nx, species, cz), F32)
        zero_z = jnp.zeros((species, cz), F32)

        @pl.when(gx == 0)
        def _():
            buf[0, 1:ny + 1] = zero_x

        @pl.when(gx == n_gx - 1)
        def _():
            buf[nx + 1, 1:ny + 1] = zero_x

        @pl.when(gy == 0)
        def _():
            buf[1:nx + 1, 0] = zero_y

        @pl.when(gy == n_gy - 1)
        def _():
            buf[1:nx + 1, ny + 1] = zero_y

        @pl.when(gz == 0)
        def _():
            edge_recv[step, 0] = zero_z

        @pl.when(gz == n_gz - 1)
        def _():
            edge_recv[step, 1] = zero_z

    lane = iota((species, cz), 1)
    def edge_part(field, r):
        return jnp.where(lane // 2 == r, pltpu.roll(field, 2 * r + 1, 1), 0.0)

    gas_in.wait()

    def load_row(r, edges):
        field = raw[pl.ds(r, species, stride=rows), :]
        first[r // ny + 1, lax.rem(r, ny) + 1] = field
        high, low = split(field)
        pair, side = r // 2, lax.rem(r, 2)
        parts[pair, side, 0:species] = high
        parts[pair, side, species:2 * species] = low
        return edges + edge_part(field, r)

    edge_send[0] = lax.fori_loop(0, rows, load_row, jnp.zeros((species, cz), F32))
    start_faces(first, 0)
    outside_zero(first, 0)
    outside_zero(second, 1)

    lam_b[...] = jnp.broadcast_to(column(liquid[...]), (species, parcels))
    sig_b[...] = jnp.broadcast_to(column(surface[...]), (species, parcels))
    gam_b[...] = jnp.broadcast_to(column(gasrate[...]), (species, cz))
    drop_in.wait()

    def droplet_block(b, carry):
        at = pl.ds(pl.multiple_of(b * 8, 8), 8)
        lam, sig = lam_b[at], sig_b[at]
        state = drop[:, at]
        unit = jnp.zeros((DROP_STEPS, 8, parcels), F32)
        base = jnp.zeros((8, parcels), F32)
        answer = jnp.zeros((8, parcels), F32)
        for _ in range(DROP_STEPS):
            flux = sig * state[-1]
            upper = jnp.concatenate([state[1:], state[-1:]], axis=0)
            lower = jnp.concatenate([state[1:2], state[:-1]], axis=0)
            state = state + lam[None] * (upper - 2.0 * state + lower)
            state = jnp.concatenate([state[:-1], (state[-1] - flux)[None]], axis=0)
            base = base + flux
            flux = sig * (unit[-1] - 1.0)
            upper = jnp.concatenate([unit[1:], unit[-1:]], axis=0)
            lower = jnp.concatenate([jnp.zeros_like(unit[:1]), unit[:-1]], axis=0)
            unit = unit + lam[None] * (upper - 2.0 * unit + lower)
            unit = jnp.concatenate([unit[:-1], (unit[-1] - flux)[None]], axis=0)
            answer = answer + flux
        drop[:, at] = state
        reply_b[:, at] = unit
        emit_b[0, at] = base
        emit_b[1, at] = answer
        return carry

    lax.fori_loop(0, species // 8, droplet_block, 0)
    inner = pl.ds(0, nodes - DROP_STEPS)
    tail = pl.ds(nodes - DROP_STEPS, DROP_STEPS)
    drop_done = pltpu.make_async_copy(drop.at[inner], drop_out.at[inner], out_sem.at[0])
    drop_done.start()

    place = lax.rem(rank, 4) * group + own
    chosen = (iota((half, parcels), 0) == place).astype(F32)
    low_half = rank < 4
    base = emit_b[0]
    base = jnp.concatenate([jnp.where(low_half, base, 0.0), jnp.where(low_half, 0.0, base)], axis=0)
    base_send[...] = exact_dot(chosen, base, NT).reshape(4, group, 2 * species)
    exchange(slab_row(base_send), slab_row(base_recv), base_ssem, base_rsem)

    await_recv(meta_row(meta_recv), meta_rsem)
    table = meta_recv[...]
    lane_slot = lax.rem(iota((group, 128), 1), 8)
    stacked = jnp.concatenate([jnp.where(lane_slot == j, table, 0.0) for j in range(8)], axis=0)
    gather_q = (iota((16, 128), 1) // 8 == iota((16, 128), 0)).astype(F32)
    byslot = exact_dot(gather_q, stacked, NT)
    ids = (byslot[0:STENCIL] + 0.5).astype(jnp.int32)
    vals = byslot[STENCIL:]
    total = vals
    for turn in range(1, STENCIL):
        same = pltpu.roll(ids, turn, 0) == ids
        total = total + jnp.where(same, pltpu.roll(vals, turn, 0), 0.0)
    sum_v = jnp.sum(vals, axis=0, keepdims=True)
    inv_mass = jnp.where(sum_v > 0.0, 1.0 / jnp.where(sum_v > 0.0, sum_v, 1.0), 0.0)
    r_f = (ids // cz).astype(F32)
    z_f = lax.rem(ids, cz).astype(F32)
    v_high = total.astype(BF16).astype(F32)
    v_low = total - v_high
    for h in range(2):
        for k in range(STENCIL):
            for ref, val in ((zk_s, z_f), (rk_s, r_f), (vh_s, v_high), (vl_s, v_low)):
                one = val[k:k + 1, h * half:(h + 1) * half]
                ref[h, k] = jnp.broadcast_to(one, (16, half)).astype(BF16)

    zero = jnp.zeros((16, half), BF16)
    none = jnp.full((16, half), -1.0, BF16)

    def build(i, carry):
        h = lax.rem(i, 2)
        r = i // 2
        at_row = jnp.full((16, half), r.astype(F32)).astype(BF16)
        key = [jnp.where(rk_s[h, k] == at_row, zk_s[h, k], none) for k in range(STENCIL)]
        vh = [vh_s[h, k] for k in range(STENCIL)]
        vl = [vl_s[h, k] for k in range(STENCIL)]
        for chunk in range(cz // 16):
            z = (iota((16, half), 0) + chunk * 16).astype(F32).astype(BF16)
            high, low = zero, zero
            for k in reversed(range(STENCIL)):
                hit = key[k] == z
                high = jnp.where(hit, vh[k], high)
                low = jnp.where(hit, vl[k], low)
            w_hi[r, h, chunk * 16:chunk * 16 + 16] = high
            w_lo[r, h, chunk * 16:chunk * 16 + 16] = low
        return carry

    lax.fori_loop(0, 2 * rows, build, 0)

    def merged(step):
        up = edge_recv[step, 1]
        down = edge_recv[step, 0]
        even = lax.rem(lane, 2) == 0
        return jnp.where(even, pltpu.roll(up, cz - 1, 1), pltpu.roll(down, 1, 1))

    def stencil(buf, halo, r):
        x, y = r // ny + 1, lax.rem(r, ny) + 1
        mid = buf[x, y]
        beside = buf[x + 1, y] + buf[x - 1, y]
        beside = beside + buf[x, y + 1] + buf[x, y - 1]
        ends = pltpu.roll(halo, cz - 1 - 2 * r, 1)
        beside = beside + jnp.where(lane == cz - 1, ends, pltpu.roll(mid, cz - 1, 1))
        beside = beside + jnp.where(lane == 0, ends, pltpu.roll(mid, 1, 1))
        return mid + gam_b[...] * (beside - 6.0 * mid)

    await_faces(first, 0)
    halo = merged(0)

    def first_step(r, edges):
        field = stencil(first, halo, r)
        second[r // ny + 1, lax.rem(r, ny) + 1] = field
        return edges + edge_part(field, r)

    edge_send[1] = lax.fori_loop(0, rows, first_step, jnp.zeros((species, cz), F32))
    start_faces(second, 1)

    acc_s[...] = jnp.zeros_like(acc_s)
    acc2_s[...] = jnp.zeros_like(acc2_s)

    def gather(i, carry):
        lhs = jnp.concatenate([parts[i, 0], parts[i, 1]], axis=1)
        for h in range(2):
            at = slice(h * half, (h + 1) * half)
            hi = jnp.concatenate([w_hi[2 * i, h], w_hi[2 * i + 1, h]], axis=0)
            lo = jnp.concatenate([w_lo[2 * i, h], w_lo[2 * i + 1, h]], axis=0)
            acc_s[:, at] += dot(lhs, hi, NN)
            acc2_s[:, at] += dot(lhs[0:species], lo, NN)
        return carry

    lax.fori_loop(0, rows // 2, gather, 0)
    held = acc_s[0:species] + acc_s[species:] + acc2_s[...]
    gas_at = held * inv_mass
    back_send[...] = jnp.transpose(
        jnp.concatenate([gas_at[:, :half], gas_at[:, half:]], axis=0)
    ).reshape(4, group, 2 * species)
    exchange(slab_row(back_send), slab_row(back_recv), back_ssem, back_rsem)

    await_recv(slab_row(base_recv), base_rsem)
    got = jnp.transpose(base_recv[...].reshape(half, 2 * species))
    base = jnp.concatenate([got[0:species], got[species:]], axis=1)
    emitted = base + emit_b[1, :, 0:1] * gas_at
    high, low = split(emitted)
    both = jnp.concatenate([high, low], axis=0)

    await_faces(second, 1)
    halo2 = merged(1)

    def last_step(i, carry):
        hi = jnp.concatenate(
            [jnp.concatenate([w_hi[2 * i + s, 0], w_hi[2 * i + s, 1]], axis=1) for s in range(2)], axis=0
        )
        lo = jnp.concatenate(
            [jnp.concatenate([w_lo[2 * i + s, 0], w_lo[2 * i + s, 1]], axis=1) for s in range(2)], axis=0
        )
        one = dot(both, hi, NT)
        add = one[0:species] + one[species:] + dot(high, lo, NT)
        for s in range(2):
            r = 2 * i + s
            field = stencil(second, halo2, r) + add[:, s * cz:(s + 1) * cz]
            out_s[pl.ds(r, species, stride=rows), :] = field
        return carry

    lax.fori_loop(0, rows // 2, last_step, 0)
    gas_done = pltpu.make_async_copy(out_s, gas_out, out_sem.at[1])
    gas_done.start()

    await_recv(slab_row(back_recv), back_rsem)
    got = jnp.transpose(back_recv[...].reshape(half, 2 * species))
    seen = exact_dot(got, chosen, NN)
    seen = jnp.where(low_half, seen[0:species], seen[species:])
    for i in range(DROP_STEPS):
        drop[nodes - DROP_STEPS + i] = drop[nodes - DROP_STEPS + i] + reply_b[i] * seen
    tail_done = pltpu.make_async_copy(drop.at[tail], drop_out.at[tail], out_sem.at[2])
    tail_done.start()

    await_send(meta_row(meta_send), meta_ssem)
    await_send(slab_row(base_send), base_ssem)
    await_send(slab_row(back_send), back_ssem)
    drain_faces(first, 0)
    drain_faces(second, 1)
    drop_done.wait()
    gas_done.wait()
    tail_done.wait()


def on_device(gas, droplet, owner, cells, weights, mass, liquid_rate, surface_rate, gas_rate):
    n_gx, n_gy, n_gz = (lax.axis_size(a) for a in ("gx", "gy", "gz"))
    species, nx, ny, cz = gas.shape
    nodes, _, parcels = droplet.shape
    group = n_gy * n_gz
    rows = nx * ny
    half = 4 * group
    vmem = pl.BlockSpec(memory_space=pltpu.VMEM)
    anyw = pl.BlockSpec(memory_space=pl.ANY)
    dma = pltpu.SemaphoreType.DMA
    padded = pltpu.VMEM((nx + 2, ny + 2, species, cz), F32)
    slabs = pltpu.VMEM((4, group, 2 * species), F32)
    held = pltpu.VMEM((species, parcels), F32)
    onehot = pltpu.VMEM((rows, 2, cz, half), BF16)
    small = pltpu.VMEM((2, STENCIL, 16, half), BF16)
    gas_next, droplet_next = pl.pallas_call(
        functools.partial(kernel, n_gx, n_gy, n_gz, nx, ny),
        out_shape=(
            jax.ShapeDtypeStruct((species * rows, cz), F32),
            jax.ShapeDtypeStruct(droplet.shape, F32),
        ),
        in_specs=[anyw, anyw] + [vmem] * 7,
        out_specs=(anyw, anyw),
        scratch_shapes=[
            pltpu.VMEM((species * rows, cz), F32),
            padded, padded,
            pltpu.VMEM((rows // 2, 2, 2 * species, cz), BF16),
            pltpu.VMEM(droplet.shape, F32),
            held, held, pltpu.VMEM((species, cz), F32),
            pltpu.VMEM((DROP_STEPS, species, parcels), F32),
            pltpu.VMEM((2, species, parcels), F32),
            onehot, onehot, small, small, small, small,
            pltpu.VMEM((2 * species, 2 * half), F32),
            pltpu.VMEM((species, 2 * half), F32),
            pltpu.VMEM((species * rows, cz), F32),
            pltpu.VMEM((group, 128), F32), pltpu.VMEM((group, 128), F32),
            slabs, slabs, slabs, slabs,
            pltpu.VMEM((2, species, cz), F32), pltpu.VMEM((2, 2, species, cz), F32),
            dma((2,)), dma((3,)),
            dma((group,)), dma((group,)), dma((group,)), dma((group,)), dma((group,)), dma((group,)),
            dma((2, 6)), dma((2, 6)),
        ],
        compiler_params=pltpu.CompilerParams(
            collective_id=0, has_side_effects=True, vmem_limit_bytes=40 << 20
        ),
        name="spray",
    )(
        gas.reshape(species * rows, cz), droplet, owner.reshape(1, parcels), cells, weights,
        mass.reshape(1, parcels), liquid_rate.reshape(1, species), surface_rate.reshape(1, species),
        gas_rate.reshape(1, species),
    )
    return gas_next.reshape(gas.shape), droplet_next


def solution(mesh):
    return jax.shard_map(
        on_device,
        mesh=mesh,
        in_specs=(
            P(None, "gx", "gy", "gz"),
            P(None, None, ("gx", "gy", "gz")),
            P(("gx", "gy", "gz"), None),
            P(None, ("gx", "gy", "gz")),
            P(None, ("gx", "gy", "gz")),
            P(("gx", "gy", "gz")),
            P(),
            P(),
            P(),
        ),
        out_specs=(P(None, "gx", "gy", "gz"), P(None, None, ("gx", "gy", "gz"))),
        check_vma=False,
    )
```

time: 193 us -> 48 us (0.25)
  the two profiles are of different devices: /device:TPU:2 before, /device:TPU:1 now
where the time goes in v1:
time: 48 us; the launch traced here: 47.8 us
  Pallas kernels  42 us (88%)
  local copies, waits for them, and re-layouts  5.09 us (11%)
  between operations  0.7 us (1%)
    pallas_call x1, Pallas kernels, on_device(): pl.pallas_call(functools.partial(kernel, n_gx, n_gy, n_gz, nx, ny), out_s...  42 us
    unnamed x20, local copies, waits for them, and re-layouts  5.09 us

profile of v1, /device:TPU:1, one launch (start us, length us, event | category | flops | bytes accessed | tf_op | source)
XLA Modules:
  0.0 47.8 jit_solution(9593260255766548763)
XLA Ops:
  0.6 0.0 copy-start.6
  0.6 0.0 copy-start.7
  0.7 0.0 copy-start.8
  0.7 0.0 copy-start.3
  0.7 0.0 copy-start.2
  0.7 0.0 copy-start.4
  0.7 0.0 copy-start.5
  0.7 0.6 %copy-done.6 = f32[64]{0:T(128)S(1)} copy-done((f32[64]{0:T(128)S(1)}, f32[64]{0:T(128)}, u32[]{:S(2)}) %copy-start.6) | copy-done | bytes 280
  1.3 0.0 copy-done.7
  1.3 0.0 copy-done.8
  1.3 0.0 copy-done.3
  1.4 0.0 copy-done.2
  1.4 0.0 copy-done.4
  1.4 0.0 copy-done.5
  1.4 0.0 copy-start
  1.4 1.2 %copy-done = f32[64,4,8,128]{3,2,1,0:T(8,128)S(1)} copy-done((f32[64,4,8,128]{3,2,1,0:T(8,128)S(1)}, f32[64,4,8,128]{3,2,1,0:T(8,128)}, u32[]{:S(2)}) %copy-start) | copy-done | bytes 1048600
  2.6 0.0 copy-start.1
  2.6 1.2 %copy-done.1 = f32[32,64,128]{2,1,0:T(8,128)S(1)} copy-done((f32[32,64,128]{2,1,0:T(8,128)S(1)}, f32[32,64,128]{2,1,0:T(8,128)}, u32[]{:S(2)}) %copy-start.1) | copy-done | bytes 1048600
  3.8 42.0 %spray.1 = (f32[2048,128]{1,0:T(8,128)S(1)}, f32[32,64,128]{2,1,0:T(8,128)S(1)}) custom-call(f32[2048,128]{1,0:T(8,128)S(1)} %bitcast.7, f32[32,64,128]{2,1,0:T(8,128)S(1)} %copy-done.1, s32[1,128]{1,0:T(1,128)S(1)} %bitcast.9, s32[8,128]{1,0:T(8,128)S(1)} %copy-done.2, f32[8,128]{1,0:T(8,128)S(1)} %copy-done.3, f32[1,128]{1,0:T(1,128)S(1)} %bitcast.10, ...), custom_call_target="tpu_custom_call" | custom-call | tf_op jit(solution)/shard_map/spray/pallas_call | solution.py:425
  45.9 1.0 %copy.13 = f32[64,4,8,128]{3,2,1,0:T(8,128)} copy(f32[64,4,8,128]{3,2,1,0:T(8,128)S(1)} %bitcast.8) | data formatting | bytes 2097152
  46.8 1.0 %copy.14 = f32[32,64,128]{2,1,0:T(8,128)} copy(f32[32,64,128]{2,1,0:T(8,128)S(1)} %get-tuple-element.9) | data formatting | bytes 2097152
Async XLA Ops:
  0.6 0.7 %copy-start.6 = (f32[64]{0:T(128)S(1)}, f32[64]{0:T(128)}, u32[]{:S(2)}) copy-start(f32[64]{0:T(128)} %param.15) | copy-start | bytes 772
  0.6 0.7 %copy-start.7 = (f32[64]{0:T(128)S(1)}, f32[64]{0:T(128)}, u32[]{:S(2)}) copy-start(f32[64]{0:T(128)} %param.16) | copy-start | bytes 772
  0.7 0.7 %copy-start.8 = (f32[64]{0:T(128)S(1)}, f32[64]{0:T(128)}, u32[]{:S(2)}) copy-start(f32[64]{0:T(128)} %param.17) | copy-start | bytes 772
  0.7 0.7 %copy-start.3 = (f32[8,128]{1,0:T(8,128)S(1)}, f32[8,128]{1,0:T(8,128)}, u32[]{:S(2)}) copy-start(f32[8,128]{1,0:T(8,128)} %weights.1) | copy-start | bytes 12292
  0.7 0.7 %copy-start.2 = (s32[8,128]{1,0:T(8,128)S(1)}, s32[8,128]{1,0:T(8,128)}, u32[]{:S(2)}) copy-start(s32[8,128]{1,0:T(8,128)} %cells.1) | copy-start | bytes 12292
  0.7 0.7 %copy-start.4 = (s32[128,1]{0,1:T(1,128)S(1)}, s32[128,1]{0,1:T(1,128)}, u32[]{:S(2)}) copy-start(s32[128,1]{0,1:T(1,128)} %param.11) | copy-start | bytes 1540
  0.7 0.7 %copy-start.5 = (f32[128]{0:T(128)S(1)}, f32[128]{0:T(128)}, u32[]{:S(2)}) copy-start(f32[128]{0:T(128)} %param.14) | copy-start | bytes 1540
  1.4 1.2 %copy-start = (f32[64,4,8,128]{3,2,1,0:T(8,128)S(1)}, f32[64,4,8,128]{3,2,1,0:T(8,128)}, u32[]{:S(2)}) copy-start(f32[64,4,8,128]{3,2,1,0:T(8,128)} %param.9) | copy-start | bytes 3145732
  2.6 1.2 %copy-start.1 = (f32[32,64,128]{2,1,0:T(8,128)S(1)}, f32[32,64,128]{2,1,0:T(8,128)}, u32[]{:S(2)}) copy-start(f32[32,64,128]{2,1,0:T(8,128)} %droplet.1) | copy-start | bytes 3145732

commit v2 on v1

--- a/solution.py
+++ b/solution.py
@@ -44,13 +44,14 @@
 
 def kernel(
     n_gx, n_gy, n_gz, nx, ny,
-    gas, droplet, owner, cells, weights, mass, liquid, surface, gasrate,
-    gas_out, drop_out,
-    raw, first, second, parts, drop, lam_b, sig_b, gam_b, reply_b, emit_b,
-    w_hi, w_lo, zk_s, rk_s, vh_s, vl_s, acc_s, acc2_s, out_s,
+    gas, droplet, owner_in, cells_in, weights_in, mass_in, liquid_in, surface_in, gasrate_in,
+    out_s, drop,
+    owner, cells, weights, mass, liquid, surface, gasrate,
+    raw, first, second, parts, lam_b, sig_b, gam_b, reply_b, emit_b,
+    w_hi, w_lo, zk_s, rk_s, vh_s, vl_s, acc_s, acc2_s,
     meta_send, meta_recv, base_send, base_recv, back_send, back_recv,
     edge_send, edge_recv,
-    in_sem, out_sem,
+    in_sem, small_sem,
     meta_ssem, meta_rsem, base_ssem, base_rsem, back_ssem, back_rsem,
     face_ssem, face_rsem,
 ):
@@ -70,6 +71,15 @@
     def peer_id(o):
         return {"gy": o // n_gz, "gz": lax.rem(o, n_gz)}
 
+    smalls = [
+        pltpu.make_async_copy(src, dst, small_sem.at[i])
+        for i, (src, dst) in enumerate((
+            (owner_in, owner), (cells_in, cells), (weights_in, weights), (mass_in, mass),
+            (liquid_in, liquid), (surface_in, surface), (gasrate_in, gasrate),
+        ))
+    ]
+    for copy in smalls:
+        copy.start()
     gas_in = pltpu.make_async_copy(gas, raw, in_sem.at[0])
     gas_in.start()
     drop_in = pltpu.make_async_copy(droplet, drop, in_sem.at[1])
@@ -88,6 +98,8 @@
             barrier, inc=1, device_id={"gx": lax.rem(gx + step, n_gx)}, device_id_type=MESH
         )
 
+    for copy in smalls:
+        copy.wait()
     own = owner[...]
     own_col = column(own)
     before = (own_col == own) & (iota((parcels, parcels), 0) < iota((parcels, parcels), 1))
@@ -205,16 +217,19 @@
 
     gas_in.wait()
 
-    def load_row(r, edges):
-        field = raw[pl.ds(r, species, stride=rows), :]
-        first[r // ny + 1, lax.rem(r, ny) + 1] = field
-        high, low = split(field)
-        pair, side = r // 2, lax.rem(r, 2)
-        parts[pair, side, 0:species] = high
-        parts[pair, side, species:2 * species] = low
-        return edges + edge_part(field, r)
-
-    edge_send[0] = lax.fori_loop(0, rows, load_row, jnp.zeros((species, cz), F32))
+    def load_rows(x, edges):
+        for y in range(ny):
+            r = x * ny + y
+            field = raw[pl.ds(r, species, stride=rows), :]
+            first[x + 1, y + 1] = field
+            high, low = split(field)
+            pair = x * (ny // 2) + y // 2
+            parts[pair, y % 2, 0:species] = high
+            parts[pair, y % 2, species:2 * species] = low
+            edges = edges + edge_part(field, r)
+        return edges
+
+    edge_send[0] = lax.fori_loop(0, nx, load_rows, jnp.zeros((species, cz), F32))
     start_faces(first, 0)
     outside_zero(first, 0)
     outside_zero(second, 1)
@@ -251,11 +266,6 @@
         return carry
 
     lax.fori_loop(0, species // 8, droplet_block, 0)
-    inner = pl.ds(0, nodes - DROP_STEPS)
-    tail = pl.ds(nodes - DROP_STEPS, DROP_STEPS)
-    drop_done = pltpu.make_async_copy(drop.at[inner], drop_out.at[inner], out_sem.at[0])
-    drop_done.start()
-
     place = lax.rem(rank, 4) * group + own
     chosen = (iota((half, parcels), 0) == place).astype(F32)
     low_half = rank < 4
@@ -286,18 +296,20 @@
         for k in range(STENCIL):
             for ref, val in ((zk_s, z_f), (rk_s, r_f), (vh_s, v_high), (vl_s, v_low)):
                 one = val[k:k + 1, h * half:(h + 1) * half]
-                ref[h, k] = jnp.broadcast_to(one, (16, half)).astype(BF16)
+                ref[h, k] = jnp.broadcast_to(one, (8, half))
 
     zero = jnp.zeros((16, half), BF16)
-    none = jnp.full((16, half), -1.0, BF16)
+
+    def twice(value):
+        return jnp.concatenate([value, value], axis=0).astype(BF16)
 
     def build(i, carry):
         h = lax.rem(i, 2)
         r = i // 2
-        at_row = jnp.full((16, half), r.astype(F32)).astype(BF16)
-        key = [jnp.where(rk_s[h, k] == at_row, zk_s[h, k], none) for k in range(STENCIL)]
-        vh = [vh_s[h, k] for k in range(STENCIL)]
-        vl = [vl_s[h, k] for k in range(STENCIL)]
+        at_row = jnp.full((8, half), r.astype(F32))
+        key = [twice(jnp.where(rk_s[h, k] == at_row, zk_s[h, k], -1.0)) for k in range(STENCIL)]
+        vh = [twice(vh_s[h, k]) for k in range(STENCIL)]
+        vl = [twice(vl_s[h, k]) for k in range(STENCIL)]
         for chunk in range(cz // 16):
             z = (iota((16, half), 0) + chunk * 16).astype(F32).astype(BF16)
             high, low = zero, zero
@@ -317,8 +329,9 @@
         even = lax.rem(lane, 2) == 0
         return jnp.where(even, pltpu.roll(up, cz - 1, 1), pltpu.roll(down, 1, 1))
 
-    def stencil(buf, halo, r):
-        x, y = r // ny + 1, lax.rem(r, ny) + 1
+    def stencil(buf, halo, x, y):
+        r = x * ny + y
+        x, y = x + 1, y + 1
         mid = buf[x, y]
         beside = buf[x + 1, y] + buf[x - 1, y]
         beside = beside + buf[x, y + 1] + buf[x, y - 1]
@@ -330,28 +343,35 @@
     await_faces(first, 0)
     halo = merged(0)
 
-    def first_step(r, edges):
-        field = stencil(first, halo, r)
-        second[r // ny + 1, lax.rem(r, ny) + 1] = field
-        return edges + edge_part(field, r)
-
-    edge_send[1] = lax.fori_loop(0, rows, first_step, jnp.zeros((species, cz), F32))
+    def first_step(x, edges):
+        for y in range(ny):
+            field = stencil(first, halo, x, y)
+            second[x + 1, y + 1] = field
+            edges = edges + edge_part(field, x * ny + y)
+        return edges
+
+    edge_send[1] = lax.fori_loop(0, nx, first_step, jnp.zeros((species, cz), F32))
     start_faces(second, 1)
 
     acc_s[...] = jnp.zeros_like(acc_s)
     acc2_s[...] = jnp.zeros_like(acc2_s)
 
-    def gather(i, carry):
-        lhs = jnp.concatenate([parts[i, 0], parts[i, 1]], axis=1)
+    def gather(g, carry):
         for h in range(2):
             at = slice(h * half, (h + 1) * half)
-            hi = jnp.concatenate([w_hi[2 * i, h], w_hi[2 * i + 1, h]], axis=0)
-            lo = jnp.concatenate([w_lo[2 * i, h], w_lo[2 * i + 1, h]], axis=0)
-            acc_s[:, at] += dot(lhs, hi, NN)
-            acc2_s[:, at] += dot(lhs[0:species], lo, NN)
+            one, two = acc_s[:, at], acc2_s[:, at]
+            for k in range(4):
+                i = 4 * g + k
+                lhs = jnp.concatenate([parts[i, 0], parts[i, 1]], axis=1)
+                hi = jnp.concatenate([w_hi[2 * i, h], w_hi[2 * i + 1, h]], axis=0)
+                lo = jnp.concatenate([w_lo[2 * i, h], w_lo[2 * i + 1, h]], axis=0)
+                one = one + dot(lhs, hi, NN)
+                two = two + dot(lhs[0:species], lo, NN)
+            acc_s[:, at] = one
+            acc2_s[:, at] = two
         return carry
 
-    lax.fori_loop(0, rows // 2, gather, 0)
+    lax.fori_loop(0, rows // 8, gather, 0)
     held = acc_s[0:species] + acc_s[species:] + acc2_s[...]
     gas_at = held * inv_mass
     back_send[...] = jnp.transpose(
@@ -369,24 +389,23 @@
     await_faces(second, 1)
     halo2 = merged(1)
 
-    def last_step(i, carry):
-        hi = jnp.concatenate(
-            [jnp.concatenate([w_hi[2 * i + s, 0], w_hi[2 * i + s, 1]], axis=1) for s in range(2)], axis=0
-        )
-        lo = jnp.concatenate(
-            [jnp.concatenate([w_lo[2 * i + s, 0], w_lo[2 * i + s, 1]], axis=1) for s in range(2)], axis=0
-        )
-        one = dot(both, hi, NT)
-        add = one[0:species] + one[species:] + dot(high, lo, NT)
-        for s in range(2):
-            r = 2 * i + s
-            field = stencil(second, halo2, r) + add[:, s * cz:(s + 1) * cz]
-            out_s[pl.ds(r, species, stride=rows), :] = field
+    def last_step(x, carry):
+        for k in range(ny // 2):
+            i = x * (ny // 2) + k
+            hi = jnp.concatenate(
+                [jnp.concatenate([w_hi[2 * i + t, 0], w_hi[2 * i + t, 1]], axis=1) for t in range(2)], axis=0
+            )
+            lo = jnp.concatenate(
+                [jnp.concatenate([w_lo[2 * i + t, 0], w_lo[2 * i + t, 1]], axis=1) for t in range(2)], axis=0
+            )
+            one = dot(both, hi, NT)
+            add = one[0:species] + one[species:] + dot(high, lo, NT)
+            for t in range(2):
+                field = stencil(second, halo2, x, 2 * k + t) + add[:, t * cz:(t + 1) * cz]
+                out_s[pl.ds(2 * i + t, species, stride=rows), :] = field
         return carry
 
-    lax.fori_loop(0, rows // 2, last_step, 0)
-    gas_done = pltpu.make_async_copy(out_s, gas_out, out_sem.at[1])
-    gas_done.start()
+    lax.fori_loop(0, nx, last_step, 0)
 
     await_recv(slab_row(back_recv), back_rsem)
     got = jnp.transpose(back_recv[...].reshape(half, 2 * species))
@@ -394,17 +413,12 @@
     seen = jnp.where(low_half, seen[0:species], seen[species:])
     for i in range(DROP_STEPS):
         drop[nodes - DROP_STEPS + i] = drop[nodes - DROP_STEPS + i] + reply_b[i] * seen
-    tail_done = pltpu.make_async_copy(drop.at[tail], drop_out.at[tail], out_sem.at[2])
-    tail_done.start()
 
     await_send(meta_row(meta_send), meta_ssem)
     await_send(slab_row(base_send), base_ssem)
     await_send(slab_row(back_send), back_ssem)
     drain_faces(first, 0)
     drain_faces(second, 1)
-    drop_done.wait()
-    gas_done.wait()
-    tail_done.wait()
 
 
 def on_device(gas, droplet, owner, cells, weights, mass, liquid_rate, surface_rate, gas_rate):
@@ -415,37 +429,38 @@
     rows = nx * ny
     half = 4 * group
     vmem = pl.BlockSpec(memory_space=pltpu.VMEM)
-    anyw = pl.BlockSpec(memory_space=pl.ANY)
+    hbm = pl.BlockSpec(memory_space=pltpu.MemorySpace.HBM)
     dma = pltpu.SemaphoreType.DMA
     padded = pltpu.VMEM((nx + 2, ny + 2, species, cz), F32)
     slabs = pltpu.VMEM((4, group, 2 * species), F32)
     held = pltpu.VMEM((species, parcels), F32)
     onehot = pltpu.VMEM((rows, 2, cz, half), BF16)
-    small = pltpu.VMEM((2, STENCIL, 16, half), BF16)
+    small = pltpu.VMEM((2, STENCIL, 8, half), F32)
     gas_next, droplet_next = pl.pallas_call(
         functools.partial(kernel, n_gx, n_gy, n_gz, nx, ny),
         out_shape=(
             jax.ShapeDtypeStruct((species * rows, cz), F32),
             jax.ShapeDtypeStruct(droplet.shape, F32),
         ),
-        in_specs=[anyw, anyw] + [vmem] * 7,
-        out_specs=(anyw, anyw),
+        in_specs=[hbm] * 9,
+        out_specs=(vmem, vmem),
         scratch_shapes=[
+            pltpu.VMEM((1, parcels), jnp.int32), pltpu.VMEM((STENCIL, parcels), jnp.int32),
+            pltpu.VMEM((STENCIL, parcels), F32), pltpu.VMEM((1, parcels), F32),
+            pltpu.VMEM((1, species), F32), pltpu.VMEM((1, species), F32), pltpu.VMEM((1, species), F32),
             pltpu.VMEM((species * rows, cz), F32),
             padded, padded,
             pltpu.VMEM((rows // 2, 2, 2 * species, cz), BF16),
-            pltpu.VMEM(droplet.shape, F32),
             held, held, pltpu.VMEM((species, cz), F32),
             pltpu.VMEM((DROP_STEPS, species, parcels), F32),
             pltpu.VMEM((2, species, parcels), F32),
             onehot, onehot, small, small, small, small,
             pltpu.VMEM((2 * species, 2 * half), F32),
             pltpu.VMEM((species, 2 * half), F32),
-            pltpu.VMEM((species * rows, cz), F32),
             pltpu.VMEM((group, 128), F32), pltpu.VMEM((group, 128), F32),
             slabs, slabs, slabs, slabs,
             pltpu.VMEM((2, species, cz), F32), pltpu.VMEM((2, 2, species, cz), F32),
-            dma((2,)), dma((3,)),
+            dma((2,)), dma((7,)),
             dma((group,)), dma((group,)), dma((group,)), dma((group,)), dma((group,)), dma((group,)),
             dma((2, 6)), dma((2, 6)),
         ],
@@ -453,11 +468,14 @@
             collective_id=0, has_side_effects=True, vmem_limit_bytes=40 << 20
         ),
         name="spray",
-    )(
-        gas.reshape(species * rows, cz), droplet, owner.reshape(1, parcels), cells, weights,
-        mass.reshape(1, parcels), liquid_rate.reshape(1, species), surface_rate.reshape(1, species),
-        gas_rate.reshape(1, species),
-    )
+    )(*(
+        pltpu.with_memory_space_constraint(a, pltpu.MemorySpace.HBM)
+        for a in (
+            gas.reshape(species * rows, cz), droplet, owner.reshape(1, parcels), cells, weights,
+            mass.reshape(1, parcels), liquid_rate.reshape(1, species), surface_rate.reshape(1, species),
+            gas_rate.reshape(1, species),
+        )
+    ))
     return gas_next.reshape(gas.shape), droplet_next
 
 

time: 48 us -> 36.6 us (0.76)
  the two profiles are of different devices: /device:TPU:1 before, /device:TPU:2 now
where the time goes in v2:
time: 36.6 us; the launch traced here: 36.3 us
  Pallas kernels  33.7 us (92%)
  local copies, waits for them, and re-layouts  1.94 us (5%)
  between operations  0.64 us (2%)
    pallas_call x1, Pallas kernels, on_device(): pl.pallas_call(functools.partial(kernel, n_gx, n_gy, n_gz, nx, ny), out_s...  33.7 us
    unnamed x2, local copies, waits for them, and re-layouts  1.94 us

profile of v2, /device:TPU:2, one launch (start us, length us, event | category | flops | bytes accessed | tf_op | source)
XLA Modules:
  0.0 36.3 jit_solution(10545268628422396735)
XLA Ops:
  0.6 33.7 %spray.1 = (f32[2048,128]{1,0:T(8,128)S(1)}, f32[32,64,128]{2,1,0:T(8,128)S(1)}) custom-call(f32[2048,128]{1,0:T(8,128)} %bitcast.8, f32[32,64,128]{2,1,0:T(8,128)} %droplet.1, s32[1,128]{1,0:T(1,128)} %bitcast.9, s32[8,128]{1,0:T(8,128)} %cells_in.1, f32[8,128]{1,0:T(8,128)} %weights_in.1, f32[1,128]{1,0:T(1,128)} %bitcast.10, f32[1,64]{1,0:T(1,128)} %bitcast.11, ...), custom_call_target="tpu_custom_call" | custom-call | tf_op jit(solution)/shard_map/spray/pallas_call | solution.py:439
  34.3 1.0 %copy.13 = f32[64,4,8,128]{3,2,1,0:T(8,128)} copy(f32[64,4,8,128]{3,2,1,0:T(8,128)S(1)} %bitcast.7) | data formatting | bytes 2097152
  35.3 1.0 %copy.14 = f32[32,64,128]{2,1,0:T(8,128)} copy(f32[32,64,128]{2,1,0:T(8,128)S(1)} %get-tuple-element.9) | data formatting | bytes 2097152

commit v3 on v2

--- a/solution.py
+++ b/solution.py
@@ -68,8 +68,21 @@
     gz = lax.axis_index("gz")
     me = gy * n_gz + gz
 
-    def peer_id(o):
-        return {"gy": o // n_gz, "gz": lax.rem(o, n_gz)}
+    shifted_z = [lax.rem(gz + b, n_gz) for b in range(n_gz)]
+
+    def each_peer(act):
+        def turn(a, carry):
+            to_y = lax.rem(gy + a, n_gy)
+            for b in range(n_gz):
+                to_z = shifted_z[b]
+                run = functools.partial(act, to_y * n_gz + to_z, {"gy": to_y, "gz": to_z})
+                if b == 0:
+                    pl.when(a > 0)(run)
+                else:
+                    run()
+            return carry
+
+        lax.fori_loop(0, n_gy, turn, 0)
 
     smalls = [
         pltpu.make_async_copy(src, dst, small_sem.at[i])
@@ -87,12 +100,9 @@
 
     barrier = pltpu.get_barrier_semaphore()
 
-    def greet(j, carry):
-        o = lax.rem(me + j, group)
-        pl.semaphore_signal(barrier, inc=1, device_id=peer_id(o), device_id_type=MESH)
-        return carry
-
-    lax.fori_loop(1, group, greet, 0)
+    each_peer(lambda o, where: pl.semaphore_signal(
+        barrier, inc=1, device_id=where, device_id_type=MESH
+    ))
     for step in (1, n_gx - 1):
         pl.semaphore_signal(
             barrier, inc=1, device_id={"gx": lax.rem(gx + step, n_gx)}, device_id_type=MESH
@@ -119,31 +129,16 @@
     pl.semaphore_wait(barrier, group + 1)
 
     def exchange(src_of, dst_of, ssem, rsem):
-        def send(j, carry):
-            o = lax.rem(me + j, group)
-            pltpu.make_async_remote_copy(
-                src_ref=src_of(o), dst_ref=dst_of(me), send_sem=ssem.at[o], recv_sem=rsem.at[me],
-                device_id=peer_id(o), device_id_type=MESH,
-            ).start()
-            return carry
-
-        lax.fori_loop(1, group, send, 0)
-        pltpu.make_async_copy(src_of(me), dst_of(me), rsem.at[me]).start()
-
-    def await_recv(dst_of, rsem):
-        def take(o, carry):
-            pltpu.make_async_copy(dst_of(o), dst_of(o), rsem.at[o]).wait()
-            return carry
-
-        lax.fori_loop(0, group, take, 0)
-
-    def await_send(src_of, ssem):
-        def take(j, carry):
-            o = lax.rem(me + j, group)
-            pltpu.make_async_copy(src_of(o), src_of(o), ssem.at[o]).wait()
-            return carry
-
-        lax.fori_loop(1, group, take, 0)
+        each_peer(lambda o, where: pltpu.make_async_remote_copy(
+            src_ref=src_of(o), dst_ref=dst_of(me), send_sem=ssem, recv_sem=rsem,
+            device_id=where, device_id_type=MESH,
+        ).start())
+        pltpu.make_async_copy(src_of(me), dst_of(me), rsem).start()
+
+    def await_all(ref, sem):
+        pltpu.make_async_copy(ref, ref, sem).wait()
+
+    most = pl.ds(0, group - 1)
 
     meta_row = lambda ref: (lambda o: ref.at[pl.ds(o, 1)])
     slab_row = lambda ref: (lambda o: ref.at[:, pl.ds(o, 1)])
@@ -274,7 +269,7 @@
     base_send[...] = exact_dot(chosen, base, NT).reshape(4, group, 2 * species)
     exchange(slab_row(base_send), slab_row(base_recv), base_ssem, base_rsem)
 
-    await_recv(meta_row(meta_recv), meta_rsem)
+    await_all(meta_recv, meta_rsem)
     table = meta_recv[...]
     lane_slot = lax.rem(iota((group, 128), 1), 8)
     stacked = jnp.concatenate([jnp.where(lane_slot == j, table, 0.0) for j in range(8)], axis=0)
@@ -303,9 +298,7 @@
     def twice(value):
         return jnp.concatenate([value, value], axis=0).astype(BF16)
 
-    def build(i, carry):
-        h = lax.rem(i, 2)
-        r = i // 2
+    def build(h, r, carry):
         at_row = jnp.full((8, half), r.astype(F32))
         key = [twice(jnp.where(rk_s[h, k] == at_row, zk_s[h, k], -1.0)) for k in range(STENCIL)]
         vh = [twice(vh_s[h, k]) for k in range(STENCIL)]
@@ -321,7 +314,7 @@
             w_lo[r, h, chunk * 16:chunk * 16 + 16] = low
         return carry
 
-    lax.fori_loop(0, 2 * rows, build, 0)
+    lax.fori_loop(0, rows, functools.partial(build, 0), 0)
 
     def merged(step):
         up = edge_recv[step, 1]
@@ -352,6 +345,8 @@
 
     edge_send[1] = lax.fori_loop(0, nx, first_step, jnp.zeros((species, cz), F32))
     start_faces(second, 1)
+
+    lax.fori_loop(0, rows, functools.partial(build, 1), 0)
 
     acc_s[...] = jnp.zeros_like(acc_s)
     acc2_s[...] = jnp.zeros_like(acc2_s)
@@ -379,7 +374,7 @@
     ).reshape(4, group, 2 * species)
     exchange(slab_row(back_send), slab_row(back_recv), back_ssem, back_rsem)
 
-    await_recv(slab_row(base_recv), base_rsem)
+    await_all(base_recv, base_rsem)
     got = jnp.transpose(base_recv[...].reshape(half, 2 * species))
     base = jnp.concatenate([got[0:species], got[species:]], axis=1)
     emitted = base + emit_b[1, :, 0:1] * gas_at
@@ -407,16 +402,16 @@
 
     lax.fori_loop(0, nx, last_step, 0)
 
-    await_recv(slab_row(back_recv), back_rsem)
+    await_all(back_recv, back_rsem)
     got = jnp.transpose(back_recv[...].reshape(half, 2 * species))
     seen = exact_dot(got, chosen, NN)
     seen = jnp.where(low_half, seen[0:species], seen[species:])
     for i in range(DROP_STEPS):
         drop[nodes - DROP_STEPS + i] = drop[nodes - DROP_STEPS + i] + reply_b[i] * seen
 
-    await_send(meta_row(meta_send), meta_ssem)
-    await_send(slab_row(base_send), base_ssem)
-    await_send(slab_row(back_send), back_ssem)
+    await_all(meta_send.at[most], meta_ssem)
+    await_all(base_send.at[:, most], base_ssem)
+    await_all(back_send.at[:, most], back_ssem)
     drain_faces(first, 0)
     drain_faces(second, 1)
 
@@ -461,7 +456,7 @@
             slabs, slabs, slabs, slabs,
             pltpu.VMEM((2, species, cz), F32), pltpu.VMEM((2, 2, species, cz), F32),
             dma((2,)), dma((7,)),
-            dma((group,)), dma((group,)), dma((group,)), dma((group,)), dma((group,)), dma((group,)),
+            dma, dma, dma, dma, dma, dma,
             dma((2, 6)), dma((2, 6)),
         ],
         compiler_params=pltpu.CompilerParams(

time: 36.6 us -> 33.4 us (0.913)
  Pallas kernels: 33.7 us -> 30.7 us
    pallas_call x1, Pallas kernels: 33.7 us -> 30.7 us  [on_device(): pl.pallas_call(functools.partial(kernel, n_gx, n_gy, n_gz, nx, ny), out_s...]
where the time goes in v3:
time: 33.4 us; the launch traced here: 33.3 us
  Pallas kernels  30.7 us (92%)
  local copies, waits for them, and re-layouts  1.94 us (6%)
  between operations  0.64 us (2%)
    pallas_call x1, Pallas kernels, on_device(): pl.pallas_call(functools.partial(kernel, n_gx, n_gy, n_gz, nx, ny), out_s...  30.7 us
    unnamed x2, local copies, waits for them, and re-layouts  1.94 us

profile of v3, /device:TPU:2, one launch (start us, length us, event | category | flops | bytes accessed | tf_op | source)
XLA Modules:
  0.0 33.3 jit_solution(9659800256190471117)
XLA Ops:
  0.6 30.7 %spray.1 = (f32[2048,128]{1,0:T(8,128)S(1)}, f32[32,64,128]{2,1,0:T(8,128)S(1)}) custom-call(f32[2048,128]{1,0:T(8,128)} %bitcast.8, f32[32,64,128]{2,1,0:T(8,128)} %droplet.1, s32[1,128]{1,0:T(1,128)} %bitcast.9, s32[8,128]{1,0:T(8,128)} %cells_in.1, f32[8,128]{1,0:T(8,128)} %weights_in.1, f32[1,128]{1,0:T(1,128)} %bitcast.10, f32[1,64]{1,0:T(1,128)} %bitcast.11, ...), custom_call_target="tpu_custom_call" | custom-call | tf_op jit(solution)/shard_map/spray/pallas_call | solution.py:434
  31.3 1.0 %copy.13 = f32[64,4,8,128]{3,2,1,0:T(8,128)} copy(f32[64,4,8,128]{3,2,1,0:T(8,128)S(1)} %bitcast.7) | data formatting | bytes 2097152
  32.3 1.0 %copy.14 = f32[32,64,128]{2,1,0:T(8,128)} copy(f32[32,64,128]{2,1,0:T(8,128)S(1)} %get-tuple-element.9) | data formatting | bytes 2097152

commit v4 on v3

--- a/solution.py
+++ b/solution.py
@@ -298,8 +298,8 @@
     def twice(value):
         return jnp.concatenate([value, value], axis=0).astype(BF16)
 
-    def build(h, r, carry):
-        at_row = jnp.full((8, half), r.astype(F32))
+    def build(h, r):
+        at_row = jnp.full((8, half), jnp.asarray(r).astype(F32))
         key = [twice(jnp.where(rk_s[h, k] == at_row, zk_s[h, k], -1.0)) for k in range(STENCIL)]
         vh = [twice(vh_s[h, k]) for k in range(STENCIL)]
         vl = [twice(vl_s[h, k]) for k in range(STENCIL)]
@@ -312,9 +312,32 @@
                 low = jnp.where(hit, vl[k], low)
             w_hi[r, h, chunk * 16:chunk * 16 + 16] = high
             w_lo[r, h, chunk * 16:chunk * 16 + 16] = low
-        return carry
-
-    lax.fori_loop(0, rows, functools.partial(build, 0), 0)
+
+    def product(h, i):
+        at = slice(h * half, (h + 1) * half)
+        lhs = jnp.concatenate([parts[i, 0], parts[i, 1]], axis=1)
+        hi = jnp.concatenate([w_hi[2 * i, h], w_hi[2 * i + 1, h]], axis=0)
+        lo = jnp.concatenate([w_lo[2 * i, h], w_lo[2 * i + 1, h]], axis=0)
+        acc_s[:, at] += dot(lhs, hi, NN)
+        acc2_s[:, at] += dot(lhs[0:species], lo, NN)
+
+    def gather_half(h):
+        build(h, 0)
+        build(h, 1)
+
+        def pair(i, carry):
+            product(h, i - 1)
+            build(h, 2 * i)
+            build(h, 2 * i + 1)
+            return carry
+
+        lax.fori_loop(1, rows // 2, pair, 0)
+        product(h, rows // 2 - 1)
+
+    acc_s[...] = jnp.zeros_like(acc_s)
+    acc2_s[...] = jnp.zeros_like(acc2_s)
+
+    gather_half(0)
 
     def merged(step):
         up = edge_recv[step, 1]
@@ -346,27 +369,7 @@
     edge_send[1] = lax.fori_loop(0, nx, first_step, jnp.zeros((species, cz), F32))
     start_faces(second, 1)
 
-    lax.fori_loop(0, rows, functools.partial(build, 1), 0)
-
-    acc_s[...] = jnp.zeros_like(acc_s)
-    acc2_s[...] = jnp.zeros_like(acc2_s)
-
-    def gather(g, carry):
-        for h in range(2):
-            at = slice(h * half, (h + 1) * half)
-            one, two = acc_s[:, at], acc2_s[:, at]
-            for k in range(4):
-                i = 4 * g + k
-                lhs = jnp.concatenate([parts[i, 0], parts[i, 1]], axis=1)
-                hi = jnp.concatenate([w_hi[2 * i, h], w_hi[2 * i + 1, h]], axis=0)
-                lo = jnp.concatenate([w_lo[2 * i, h], w_lo[2 * i + 1, h]], axis=0)
-                one = one + dot(lhs, hi, NN)
-                two = two + dot(lhs[0:species], lo, NN)
-            acc_s[:, at] = one
-            acc2_s[:, at] = two
-        return carry
-
-    lax.fori_loop(0, rows // 8, gather, 0)
+    gather_half(1)
     held = acc_s[0:species] + acc_s[species:] + acc2_s[...]
     gas_at = held * inv_mass
     back_send[...] = jnp.transpose(
@@ -414,6 +417,19 @@
     await_all(back_send.at[:, most], back_ssem)
     drain_faces(first, 0)
     drain_faces(second, 1)
+
+
+def store(gas, droplet, gas_out, drop_out, sem):
+    copies = []
+    for i, (src, dst) in enumerate(((gas, gas_out), (droplet, drop_out))):
+        step = src.shape[0] // 4
+        for k in range(4):
+            at = pl.ds(k * step, step)
+            copies.append(pltpu.make_async_copy(src.at[at], dst.at[at], sem.at[i, k]))
+    for copy in copies:
+        copy.start()
+    for copy in copies:
+        copy.wait()
 
 
 def on_device(gas, droplet, owner, cells, weights, mass, liquid_rate, surface_rate, gas_rate):
@@ -471,6 +487,19 @@
             gas_rate.reshape(1, species),
         )
     ))
+    gas_next, droplet_next = pl.pallas_call(
+        store,
+        out_shape=(
+            jax.ShapeDtypeStruct((species * rows, cz), F32),
+            jax.ShapeDtypeStruct(droplet.shape, F32),
+        ),
+        in_specs=[vmem, vmem],
+        out_specs=(hbm, hbm),
+        scratch_shapes=[dma((2, 4))],
+        name="store",
+    )(*(
+        pltpu.with_memory_space_constraint(a, pltpu.MemorySpace.VMEM) for a in (gas_next, droplet_next)
+    ))
     return gas_next.reshape(gas.shape), droplet_next
 
 

time: 33.4 us -> 34.2 us (1.024)
  Pallas kernels: 30.7 us -> 33.4 us
  local copies, waits for them, and re-layouts: 1.94 us -> 0 us
    unnamed x2 -> x0, local copies, waits for them, and re-layouts: 1.94 us -> none
    pallas_call x1, Pallas kernels: 30.7 us -> 32.1 us  [on_device(): pl.pallas_call(functools.partial(kernel, n_gx, n_gy, n_gz, nx, ny), out_s...]
    pallas_call x0 -> x1, Pallas kernels: none -> 1.38 us  [on_device(): pl.pallas_call(store, out_shape=(jax.ShapeDtypeStruct((species * rows, cz...]
where the time goes in v4:
time: 34.2 us; the launch traced here: 34.1 us
  Pallas kernels  33.4 us (98%)
  between operations  0.64 us (2%)
    pallas_call x1, Pallas kernels, on_device(): pl.pallas_call(functools.partial(kernel, n_gx, n_gy, n_gz, nx, ny), out_s...  32.1 us
    pallas_call x1, Pallas kernels, on_device(): pl.pallas_call(store, out_shape=(jax.ShapeDtypeStruct((species * rows, cz...  1.38 us

profile of v4, /device:TPU:2, one launch (start us, length us, event | category | flops | bytes accessed | tf_op | source)
XLA Modules:
  0.0 34.1 jit_solution(8431556072082563986)
XLA Ops:
  0.6 32.1 %spray.1 = (f32[2048,128]{1,0:T(8,128)S(1)}, f32[32,64,128]{2,1,0:T(8,128)S(1)}) custom-call(f32[2048,128]{1,0:T(8,128)} %bitcast.7, f32[32,64,128]{2,1,0:T(8,128)} %droplet.1, s32[1,128]{1,0:T(1,128)} %bitcast.8, s32[8,128]{1,0:T(8,128)} %cells_in.1, f32[8,128]{1,0:T(8,128)} %weights_in.1, f32[1,128]{1,0:T(1,128)} %bitcast.9, f32[1,64]{1,0:T(1,128)} %bitcast.10, ...), custom_call_target="tpu_custom_call" | custom-call | tf_op jit(solution)/shard_map/spray/pallas_call | solution.py:450
  32.7 1.4 %store.1 = (f32[2048,128]{1,0:T(8,128)}, f32[32,64,128]{2,1,0:T(8,128)}) custom-call(f32[2048,128]{1,0:T(8,128)S(1)} %get-tuple-element.6.gas, f32[32,64,128]{2,1,0:T(8,128)S(1)} %get-tuple-element.7.droplet), custom_call_target="tpu_custom_call" | custom-call | tf_op jit(solution)/shard_map/store/pallas_call | solution.py:490

commit v5 on v3

--- a/solution.py
+++ b/solution.py
@@ -298,7 +298,7 @@
     def twice(value):
         return jnp.concatenate([value, value], axis=0).astype(BF16)
 
-    def build(h, r, carry):
+    def build_row(h, r):
         at_row = jnp.full((8, half), r.astype(F32))
         key = [twice(jnp.where(rk_s[h, k] == at_row, zk_s[h, k], -1.0)) for k in range(STENCIL)]
         vh = [twice(vh_s[h, k]) for k in range(STENCIL)]
@@ -312,9 +312,11 @@
                 low = jnp.where(hit, vl[k], low)
             w_hi[r, h, chunk * 16:chunk * 16 + 16] = high
             w_lo[r, h, chunk * 16:chunk * 16 + 16] = low
+
+    def build(h, i, carry):
+        build_row(h, 2 * i)
+        build_row(h, 2 * i + 1)
         return carry
-
-    lax.fori_loop(0, rows, functools.partial(build, 0), 0)
 
     def merged(step):
         up = edge_recv[step, 1]
@@ -345,8 +347,10 @@
 
     edge_send[1] = lax.fori_loop(0, nx, first_step, jnp.zeros((species, cz), F32))
     start_faces(second, 1)
-
-    lax.fori_loop(0, rows, functools.partial(build, 1), 0)
+    lax.fori_loop(0, rows // 2, functools.partial(build, 0), 0)
+
+
+    lax.fori_loop(0, rows // 2, functools.partial(build, 1), 0)
 
     acc_s[...] = jnp.zeros_like(acc_s)
     acc2_s[...] = jnp.zeros_like(acc2_s)
@@ -355,8 +359,8 @@
         for h in range(2):
             at = slice(h * half, (h + 1) * half)
             one, two = acc_s[:, at], acc2_s[:, at]
-            for k in range(4):
-                i = 4 * g + k
+            for k in range(8):
+                i = 8 * g + k
                 lhs = jnp.concatenate([parts[i, 0], parts[i, 1]], axis=1)
                 hi = jnp.concatenate([w_hi[2 * i, h], w_hi[2 * i + 1, h]], axis=0)
                 lo = jnp.concatenate([w_lo[2 * i, h], w_lo[2 * i + 1, h]], axis=0)
@@ -366,7 +370,7 @@
             acc2_s[:, at] = two
         return carry
 
-    lax.fori_loop(0, rows // 8, gather, 0)
+    lax.fori_loop(0, rows // 16, gather, 0)
     held = acc_s[0:species] + acc_s[species:] + acc2_s[...]
     gas_at = held * inv_mass
     back_send[...] = jnp.transpose(
@@ -414,6 +418,19 @@
     await_all(back_send.at[:, most], back_ssem)
     drain_faces(first, 0)
     drain_faces(second, 1)
+
+
+def store(gas, droplet, gas_out, drop_out, sem):
+    copies = []
+    for i, (src, dst) in enumerate(((gas, gas_out), (droplet, drop_out))):
+        step = src.shape[0] // 4
+        for k in range(4):
+            at = pl.ds(k * step, step)
+            copies.append(pltpu.make_async_copy(src.at[at], dst.at[at], sem.at[i, k]))
+    for copy in copies:
+        copy.start()
+    for copy in copies:
+        copy.wait()
 
 
 def on_device(gas, droplet, owner, cells, weights, mass, liquid_rate, surface_rate, gas_rate):
@@ -471,6 +488,19 @@
             gas_rate.reshape(1, species),
         )
     ))
+    gas_next, droplet_next = pl.pallas_call(
+        store,
+        out_shape=(
+            jax.ShapeDtypeStruct((species * rows, cz), F32),
+            jax.ShapeDtypeStruct(droplet.shape, F32),
+        ),
+        in_specs=[vmem, vmem],
+        out_specs=(hbm, hbm),
+        scratch_shapes=[dma((2, 4))],
+        name="store",
+    )(*(
+        pltpu.with_memory_space_constraint(a, pltpu.MemorySpace.VMEM) for a in (gas_next, droplet_next)
+    ))
     return gas_next.reshape(gas.shape), droplet_next
 
 

time: 33.4 us -> 32 us (0.958)
  local copies, waits for them, and re-layouts: 1.94 us -> 0 us
  Pallas kernels: 30.7 us -> 31.2 us
    unnamed x2 -> x0, local copies, waits for them, and re-layouts: 1.94 us -> none
    pallas_call x0 -> x1, Pallas kernels: none -> 1.38 us  [on_device(): pl.pallas_call(store, out_shape=(jax.ShapeDtypeStruct((species * rows, cz...]
    pallas_call x1, Pallas kernels: 30.7 us -> 29.8 us  [on_device(): pl.pallas_call(functools.partial(kernel, n_gx, n_gy, n_gz, nx, ny), out_s...]
where the time goes in v5:
time: 32 us; the launch traced here: 31.9 us
  Pallas kernels  31.2 us (98%)
  between operations  0.64 us (2%)
    pallas_call x1, Pallas kernels, on_device(): pl.pallas_call(functools.partial(kernel, n_gx, n_gy, n_gz, nx, ny), out_s...  29.8 us
    pallas_call x1, Pallas kernels, on_device(): pl.pallas_call(store, out_shape=(jax.ShapeDtypeStruct((species * rows, cz...  1.38 us

profile of v5, /device:TPU:2, one launch (start us, length us, event | category | flops | bytes accessed | tf_op | source)
XLA Modules:
  0.0 31.9 jit_solution(98630318213369343)
XLA Ops:
  0.6 29.8 %spray.1 = (f32[2048,128]{1,0:T(8,128)S(1)}, f32[32,64,128]{2,1,0:T(8,128)S(1)}) custom-call(f32[2048,128]{1,0:T(8,128)} %bitcast.7, f32[32,64,128]{2,1,0:T(8,128)} %droplet.1, s32[1,128]{1,0:T(1,128)} %bitcast.8, s32[8,128]{1,0:T(8,128)} %cells_in.1, f32[8,128]{1,0:T(8,128)} %weights_in.1, f32[1,128]{1,0:T(1,128)} %bitcast.9, f32[1,64]{1,0:T(1,128)} %bitcast.10, ...), custom_call_target="tpu_custom_call" | custom-call | tf_op jit(solution)/shard_map/spray/pallas_call | solution.py:451
  30.5 1.4 %store.1 = (f32[2048,128]{1,0:T(8,128)}, f32[32,64,128]{2,1,0:T(8,128)}) custom-call(f32[2048,128]{1,0:T(8,128)S(1)} %get-tuple-element.6.gas, f32[32,64,128]{2,1,0:T(8,128)S(1)} %get-tuple-element.7.droplet), custom_call_target="tpu_custom_call" | custom-call | tf_op jit(solution)/shard_map/store/pallas_call | solution.py:491

commit v6 on v5

--- a/solution.py
+++ b/solution.py
@@ -148,12 +148,12 @@
     def faces(buf, step):
         inner_x, inner_y = pl.ds(1, nx), pl.ds(1, ny)
         table = [
-            (gx > 0, {"gx": gx - 1}, buf.at[1, inner_y], buf.at[nx + 1, inner_y], gx < n_gx - 1),
-            (gx < n_gx - 1, {"gx": gx + 1}, buf.at[nx, inner_y], buf.at[0, inner_y], gx > 0),
             (gy > 0, {"gy": gy - 1}, buf.at[inner_x, 1], buf.at[inner_x, ny + 1], gy < n_gy - 1),
             (gy < n_gy - 1, {"gy": gy + 1}, buf.at[inner_x, ny], buf.at[inner_x, 0], gy > 0),
             (gz > 0, {"gz": gz - 1}, edge_send.at[step], edge_recv.at[step, 1], gz < n_gz - 1),
             (gz < n_gz - 1, {"gz": gz + 1}, edge_send.at[step], edge_recv.at[step, 0], gz > 0),
+            (gx > 0, {"gx": gx - 1}, buf.at[1, inner_y], buf.at[nx + 1, inner_y], gx < n_gx - 1),
+            (gx < n_gx - 1, {"gx": gx + 1}, buf.at[nx, inner_y], buf.at[0, inner_y], gx > 0),
         ]
         out = []
         for i, (send_if, target, src, dst, recv_if) in enumerate(table):
@@ -423,8 +423,8 @@
 def store(gas, droplet, gas_out, drop_out, sem):
     copies = []
     for i, (src, dst) in enumerate(((gas, gas_out), (droplet, drop_out))):
-        step = src.shape[0] // 4
-        for k in range(4):
+        step = src.shape[0] // 2
+        for k in range(2):
             at = pl.ds(k * step, step)
             copies.append(pltpu.make_async_copy(src.at[at], dst.at[at], sem.at[i, k]))
     for copy in copies:
@@ -496,7 +496,7 @@
         ),
         in_specs=[vmem, vmem],
         out_specs=(hbm, hbm),
-        scratch_shapes=[dma((2, 4))],
+        scratch_shapes=[dma((2, 2))],
         name="store",
     )(*(
         pltpu.with_memory_space_constraint(a, pltpu.MemorySpace.VMEM) for a in (gas_next, droplet_next)

time: 32 us -> 31.9 us (level)
  no operation moved by 1% of the time
where the time goes in v6:
time: 31.9 us; the launch traced here: 31.8 us
  Pallas kernels  31.2 us (98%)
  between operations  0.64 us (2%)
    pallas_call x1, Pallas kernels, on_device(): pl.pallas_call(functools.partial(kernel, n_gx, n_gy, n_gz, nx, ny), out_s...  29.8 us
    pallas_call x1, Pallas kernels, on_device(): pl.pallas_call(store, out_shape=(jax.ShapeDtypeStruct((species * rows, cz...  1.35 us

profile of v6, /device:TPU:2, one launch (start us, length us, event | category | flops | bytes accessed | tf_op | source)
XLA Modules:
  0.0 31.8 jit_solution(4628601789285618314)
XLA Ops:
  0.6 29.8 %spray.1 = (f32[2048,128]{1,0:T(8,128)S(1)}, f32[32,64,128]{2,1,0:T(8,128)S(1)}) custom-call(f32[2048,128]{1,0:T(8,128)} %bitcast.7, f32[32,64,128]{2,1,0:T(8,128)} %droplet.1, s32[1,128]{1,0:T(1,128)} %bitcast.8, s32[8,128]{1,0:T(8,128)} %cells_in.1, f32[8,128]{1,0:T(8,128)} %weights_in.1, f32[1,128]{1,0:T(1,128)} %bitcast.9, f32[1,64]{1,0:T(1,128)} %bitcast.10, ...), custom_call_target="tpu_custom_call" | custom-call | tf_op jit(solution)/shard_map/spray/pallas_call | solution.py:451
  30.5 1.3 %store.1 = (f32[2048,128]{1,0:T(8,128)}, f32[32,64,128]{2,1,0:T(8,128)}) custom-call(f32[2048,128]{1,0:T(8,128)S(1)} %get-tuple-element.6.gas, f32[32,64,128]{2,1,0:T(8,128)S(1)} %get-tuple-element.7.droplet), custom_call_target="tpu_custom_call" | custom-call | tf_op jit(solution)/shard_map/store/pallas_call | solution.py:491
